TPU v7x, 32 devices: a whole 2x2x4 slice. The times are simulated.
32 devices in a mesh: group: 2 (over x), row: 16 (over z, y, core).
Axes of the slice: x: 2, y: 2, z: 4, core: 2. Of those that a mesh axis runs over, the one named last changes fastest.
Arguments:
- near_tiles: bfloat16 [2, 5, 1024, 1024], replicated, may hold values from -0.1875 to 0.1875
- near_order: int32 [5], replicated, may hold values from 0 to 4, each once
- receiver_basis: bfloat16 [2, 1024, 16], replicated, may hold values from -1.5 to 1.5
- source_basis: bfloat16 [2, 1024, 16], replicated, may hold values from -0.1875 to 0.1875
- coupling: float32 [2, 16, 16, 16], replicated, may hold values from -0.375 to 0.375
- initial_model: bfloat16 [2, 128, 16384], P(None, 'group', 'row'), parts along dimension 1, may hold values from -6 to 6
- observed: bfloat16 [128, 16384], P('group', 'row'), parts along dimension 0, may hold values from -18 to 18
Outputs:
- model_out: float32 [2, 128, 16384], P(None, 'group', 'row'), parts along dimension 1
- misfit: float32 [128, 16384], P('group', 'row'), parts along dimension 0
There are 2 independent parts, one for each index of `group`. A program takes and returns all parts, laid end to end along the dimension named above; an argument that names none is the same for every part. Nothing has to cross between parts.
Inputs may be any that keep to these rules, and one draw needn't show every extreme that they name: `near_order`: a permutation of 0 to 4.
All inputs are finite; a program needn't handle non-finite values.
Results may differ from a plain program's by a relative error of at most 0.0029.
Values may be sent and summed in bfloat16 or wider, within the bound.
No kernel may reach another device: no remote copies, remote signals or barrier semaphores. Data moves between devices by JAX's collectives and lax.ppermute only.
A program may use at most 128 MiB of HBM per device.

v0:
```python
import jax
import jax.numpy as jnp
from jax import lax
from jax.sharding import PartitionSpec as P

RADIUS = 2
ITERS = 3


def shifted(block, axis, distance):
    devices = range(lax.axis_size(axis))
    route = [((i - distance) % len(devices), i) for i in devices]
    return lax.ppermute(block, axis, route)


def on_device(
    near_tiles, near_order, receiver_basis, source_basis, coupling, initial_model, observed
):
    highest = lax.Precision.HIGHEST
    band_count = coupling.shape[1]
    own_band = lax.axis_index("row")
    inverse = jnp.argsort(near_order)
    tile_list = [
        lax.dynamic_index_in_dim(near_tiles, inverse[offset_slot], 1, keepdims=False)
        for offset_slot in range(2 * RADIUS + 1)
    ]
    receiver_full = receiver_basis.astype(jnp.float32)
    source_full = source_basis.astype(jnp.float32)
    model = initial_model.astype(jnp.float32)
    measured = observed.astype(jnp.float32)
    layer_count, pert_count, point_count = model.shape
    misfit = measured
    for step_index in range(ITERS):
        model_wire = model.astype(jnp.bfloat16)
        received_map = {0: model_wire}
        for heading in (1, -1):
            current = model_wire
            for distance in range(1, RADIUS + 1):
                current = shifted(current, "row", heading)
                received_map[heading * distance] = current
        predicted = jnp.zeros((pert_count, point_count), jnp.float32)
        for offset_slot in range(2 * RADIUS + 1):
            shift_by = offset_slot - RADIUS
            predicted = predicted + jnp.einsum(
                "lpc,lac->pa",
                received_map[shift_by],
                tile_list[offset_slot],
                preferred_element_type=jnp.float32,
            )
        summary = jnp.einsum(
            "lpc,lcs->lsp", model_wire, source_basis, preferred_element_type=jnp.float32
        )
        add_received = lax.all_gather(summary[None], "row", axis=0, tiled=True)
        sources = jnp.arange(add_received.shape[0], dtype=jnp.int32)
        chosen = jnp.take(coupling, (own_band - sources) % band_count, axis=1)
        far_field = jnp.einsum("ljrs,jlsp->lrp", chosen, add_received, precision=highest)
        predicted = predicted + jnp.einsum(
            "lar,lrp->pa", receiver_full, far_field, precision=highest
        )
        misfit = measured - predicted
        misfit_wire = misfit.astype(jnp.bfloat16)
        gradient = jnp.zeros_like(model)
        for offset_slot in range(2 * RADIUS + 1):
            shift_by = offset_slot - RADIUS
            if shift_by == 0:
                received = misfit_wire
            else:
                received = shifted(misfit_wire, "row", -shift_by)
            gradient = gradient + jnp.einsum(
                "pa,lac->lpc", received, tile_list[offset_slot], preferred_element_type=jnp.float32
            )
        data_summary = jnp.einsum(
            "lar,pa->lrp", receiver_full, misfit_wire.astype(jnp.float32), precision=highest
        )

        def add_back(received):
            sources = jnp.arange(received.shape[0], dtype=jnp.int32)
            chosen = jnp.take(coupling, (sources - own_band) % band_count, axis=1)
            return jnp.einsum("lirs,ilrp->lsp", chosen, received, precision=highest)

        far_back = add_back(lax.all_gather(data_summary[None], "row", axis=0, tiled=True))
        gradient = gradient + jnp.einsum("lcs,lsp->lpc", source_full, far_back, precision=highest)
        model = model + 0.01 * (gradient - 10.0 * model)
    return (model, misfit)


def solution(mesh):
    placed = (P(), P(), P(), P(), P(), P(None, "group", "row"), P("group", "row"))
    return jax.shard_map(
        on_device,
        mesh=mesh,
        in_specs=placed,
        out_specs=(P(None, "group", "row"), P("group", "row")),
        check_vma=False,
    )
```

profile of v0, /device:TPU:0, one launch (start us, length us, event | category | flops | bytes accessed | tf_op | source)
XLA Modules:
  0.0 225.2 jit_solution(1642247805543370166)
XLA Ops:
  0.7 5.5 %collective-permute-start = (bf16[2,64,1024]{2,1,0:T(8,128)(2,1)}, bf16[2,64,1024]{2,1,0:T(8,128)(2,1)S(1)}, u32[]{:S(2)}, u32[]{:S(2)}) collective-permute-start(bf16[2,64,1024]{2,1,0:T(8,128)(2,1)} %param.14), channel_id=1, source_target_pairs={{1,0},{2,1},{3,2},{4,3},{5,4},{6,5},{7,6},{8,7},{9,8},{10,9},{11,1... | collective-permute-start | bytes 786440 | tf_op jit(solution)/shard_map/ppermute | solution.py:13
  11.1 18.9 %all-gather = f32[32,16,64]{2,1,0:T(8,128)S(1)} all-gather(f32[2,16,64]{2,1,0:T(8,128)S(1)} %fusion.360), channel_id=2, replica_groups=mesh['group'=2,'row'=16] {'row'}, dimensions={0}, use_global_device_ids=true | all-gather | bytes 139264 | tf_op jit(solution)/shard_map/all_gather | solution.py:53
  31.2 3.6 %fusion.189 = f32[1024,64]{0,1:T(8,128)S(1)} fusion(bf16[2,64,1024]{2,1,0:T(8,128)(2,1)} %param.14, bf16[2,5,1024,1024]{3,2,1,0:T(8,128)(2,1)} %param.9, s32[]{:T(128)S(6)} %select_n.44), kind=kOutput, calls=%fused_computation.125 | convolution fusion | flops 268435456 | bytes 4718596 | tf_op jit(solution)/shard_map/lpc,lac->pa/dot_general | solution.py:44
  46.5 3.7 %fusion.180 = f32[1024,64]{0,1:T(8,128)S(1)} fusion(bf16[2,64,1024]{2,1,0:T(8,128)(2,1)S(1)} %collective-permute-done, bf16[2,5,1024,1024]{3,2,1,0:T(8,128)(2,1)} %param.9, s32[]{:T(128)S(6)} %select_n.43), kind=kOutput, calls=%fused_computation.122 | convolution fusion | flops 268435456 | bytes 4718596 | tf_op jit(solution)/shard_map/lpc,lac->pa/dot_general | solution.py:44
  50.3 4.3 %fusion.270 = f32[1024,64]{0,1:T(8,128)S(1)} fusion(f32[1024,64]{0,1:T(8,128)S(1)} %fusion.189, f32[1024,64]{0,1:T(8,128)S(1)} %fusion.180, bf16[2,64,1024]{2,1,0:T(8,128)(2,1)S(1)} %collective-permute-done.1, bf16[2,5,1024,1024]{3,2,1,0:T(8,128)(2,1)} %param.9, s32[]{:T(128)S(6)} %select_n.42), kind=kOutput, calls=%fused_computation.155 | convolution fusion | flops 268566528 | bytes 5242884 | tf_op jit(solution)/shard_map/lpc,lac->pa/dot_general | solution.py:44
  54.6 3.9 %fusion.252 = f32[1024,64]{0,1:T(8,128)S(1)} fusion(f32[1024,64]{0,1:T(8,128)S(1)} %fusion.270, bf16[2,64,1024]{2,1,0:T(8,128)(2,1)S(1)} %collective-permute-done.2, bf16[2,5,1024,1024]{3,2,1,0:T(8,128)(2,1)} %param.9, s32[]{:T(128)S(6)} %select_n.45), kind=kOutput, calls=%fused_computation.149 | convolution fusion | flops 268500992 | bytes 4980740 | tf_op jit(solution)/shard_map/lpc,lac->pa/dot_general | solution.py:44
  58.5 3.6 %fusion.273 = bf16[64,1024]{1,0:T(8,128)(2,1)S(1)} fusion(f32[64,1024]{1,0:T(8,128)S(1)} %convolution_bitcast_fusion.2, f32[1024,64]{0,1:T(8,128)S(1)} %fusion.252, bf16[2,64,1024]{2,1,0:T(8,128)(2,1)S(1)} %collective-permute-done.3, bf16[2,5,1024,1024]{3,2,1,0:T(8,128)(2,1)} %param.9, s32[]{:T(128)S(6)} %select_n.46, bf16[64,1024]{1,0:T(8,128)(2,1)S(1)} %copy-done.5), kind=kOutput, calls=%fused_computation.156 | convolution fusion | flops 268763136 | bytes 5242884 | tf_op jit(solution)/shard_map/lpc,lac->pa/dot_general | solution.py:44
  62.6 3.7 %collective-permute-start.6 = (bf16[64,1024]{1,0:T(8,128)(2,1)S(1)}, bf16[64,1024]{1,0:T(8,128)(2,1)S(1)}, u32[]{:S(2)}, u32[]{:S(2)}) collective-permute-start(bf16[64,1024]{1,0:T(8,128)(2,1)S(1)} %fusion.273), channel_id=1, source_target_pairs={{1,0},{2,1},{3,2},{4,3},{5,4},{6,5},{7,6},{8,7},{9,8},{10,9},{11,1... | collective-permute-start | bytes 393224 | tf_op jit(solution)/shard_map/ppermute | solution.py:13
  66.3 1.6 collective-permute-start.4
  69.0 21.0 %all-gather.1 = f32[32,16,64]{2,1,0:T(8,128)S(1)} all-gather(f32[2,16,64]{2,1,0:T(8,128)S(1)} %bitcast.475), channel_id=3, replica_groups=mesh['group'=2,'row'=16] {'row'}, dimensions={0}, use_global_device_ids=true | all-gather | bytes 139264 | tf_op jit(solution)/shard_map/all_gather | solution.py:81
  97.1 19.6 %all-gather.2 = f32[32,16,64]{2,1,0:T(8,128)S(1)} all-gather(f32[2,16,64]{2,1,0:T(8,128)S(1)} %convolution_bitcast_fusion.4), channel_id=4, replica_groups=mesh['group'=2,'row'=16] {'row'}, dimensions={0}, use_global_device_ids=true | all-gather | bytes 139264 | tf_op jit(solution)/shard_map/all_gather | solution.py:53
  119.7 1.9 collective-permute-done.9
  124.5 2.2 collective-permute-done.11
  128.9 1.8 collective-permute-start.14
  130.8 1.6 collective-permute-start.12
  133.3 21.1 %all-gather.3 = f32[32,16,64]{2,1,0:T(8,128)S(1)} all-gather(f32[2,16,64]{2,1,0:T(8,128)S(1)} %bitcast.474), channel_id=5, replica_groups=mesh['group'=2,'row'=16] {'row'}, dimensions={0}, use_global_device_ids=true | all-gather | bytes 139264 | tf_op jit(solution)/shard_map/all_gather | solution.py:81
  161.3 19.7 %all-gather.4 = f32[32,16,64]{2,1,0:T(8,128)S(1)} all-gather(f32[2,16,64]{2,1,0:T(8,128)S(1)} %convolution_bitcast_fusion.3), channel_id=6, replica_groups=mesh['group'=2,'row'=16] {'row'}, dimensions={0}, use_global_device_ids=true | all-gather | bytes 139264 | tf_op jit(solution)/shard_map/all_gather | solution.py:53
  184.1 2.1 collective-permute-done.17
  189.0 2.2 collective-permute-done.19
  191.2 2.1 fusion.359
  194.2 1.8 collective-permute-start.22
  196.0 1.6 collective-permute-start.20
  198.5 21.1 %all-gather.5 = f32[32,16,64]{2,1,0:T(8,128)S(1)} all-gather(f32[2,16,64]{2,1,0:T(8,128)S(1)} %bitcast.473), channel_id=7, replica_groups=mesh['group'=2,'row'=16] {'row'}, dimensions={0}, use_global_device_ids=true | all-gather | bytes 139264 | tf_op jit(solution)/shard_map/all_gather | solution.py:81
  223.3 1.9 fusion.168
  (100 shorter events, 43.4 us)
Async XLA Ops:
  0.7 36.1 %collective-permute-start = (bf16[2,64,1024]{2,1,0:T(8,128)(2,1)}, bf16[2,64,1024]{2,1,0:T(8,128)(2,1)S(1)}, u32[]{:S(2)}, u32[]{:S(2)}) collective-permute-start(bf16[2,64,1024]{2,1,0:T(8,128)(2,1)} %param.14), channel_id=1, source_target_pairs={{1,0},{2,1},{3,2},{4,3},{5,4},{6,5},{7,6},{8,7},{9,8},{10,9},{11,1... | collective-permute-start | bytes 786440 | tf_op jit(solution)/shard_map/ppermute | solution.py:13
  6.2 40.3 %collective-permute-start.2 = (bf16[2,64,1024]{2,1,0:T(8,128)(2,1)}, bf16[2,64,1024]{2,1,0:T(8,128)(2,1)S(1)}, u32[]{:S(2)}, u32[]{:S(2)}) collective-permute-start(bf16[2,64,1024]{2,1,0:T(8,128)(2,1)} %param.14), channel_id=1, source_target_pairs={{15,0},{0,1},{1,2},{2,3},{3,4},{4,5},{5,6},{6,7},{7,8},{8,9},{9,10... | collective-permute-start | bytes 786440 | tf_op jit(solution)/shard_map/ppermute | solution.py:13
  36.8 13.5 %collective-permute-start.1 = (bf16[2,64,1024]{2,1,0:T(8,128)(2,1)S(1)}, bf16[2,64,1024]{2,1,0:T(8,128)(2,1)S(1)}, u32[]{:S(2)}, u32[]{:S(2)}) collective-permute-start(bf16[2,64,1024]{2,1,0:T(8,128)(2,1)S(1)} %collective-permute-done), channel_id=1, source_target_pairs={{1,0},{2,1},{3,2},{4,3},{5,4},{6,5},{7,6},{8,7},{9,8},{10,9},{11,1... | collective-permute-start | bytes 786440 | tf_op jit(solution)/shard_map/ppermute | solution.py:13
  46.5 12.1 %collective-permute-start.3 = (bf16[2,64,1024]{2,1,0:T(8,128)(2,1)S(1)}, bf16[2,64,1024]{2,1,0:T(8,128)(2,1)S(1)}, u32[]{:S(2)}, u32[]{:S(2)}) collective-permute-start(bf16[2,64,1024]{2,1,0:T(8,128)(2,1)S(1)} %collective-permute-done.2), channel_id=1, source_target_pairs={{15,0},{0,1},{1,2},{2,3},{3,4},{4,5},{5,6},{6,7},{7,8},{8,9},{9,10... | collective-permute-start | bytes 786440 | tf_op jit(solution)/shard_map/ppermute | solution.py:13
  62.2 30.6 %collective-permute-start.7 = (bf16[64,1024]{1,0:T(8,128)(2,1)S(1)}, bf16[64,1024]{1,0:T(8,128)(2,1)S(1)}, u32[]{:S(2)}, u32[]{:S(2)}) collective-permute-start(bf16[64,1024]{1,0:T(8,128)(2,1)S(1)} %fusion.273), channel_id=1, source_target_pairs={{2,0},{3,1},{4,2},{5,3},{6,4},{7,5},{8,6},{9,7},{10,8},{11,9},{12,... | collective-permute-start | bytes 393224 | tf_op jit(solution)/shard_map/ppermute | solution.py:13
  62.6 29.4 %collective-permute-start.6 = (bf16[64,1024]{1,0:T(8,128)(2,1)S(1)}, bf16[64,1024]{1,0:T(8,128)(2,1)S(1)}, u32[]{:S(2)}, u32[]{:S(2)}) collective-permute-start(bf16[64,1024]{1,0:T(8,128)(2,1)S(1)} %fusion.273), channel_id=1, source_target_pairs={{1,0},{2,1},{3,2},{4,3},{5,4},{6,5},{7,6},{8,7},{9,8},{10,9},{11,1... | collective-permute-start | bytes 393224 | tf_op jit(solution)/shard_map/ppermute | solution.py:13
  66.3 24.8 %collective-permute-start.5 = (bf16[64,1024]{1,0:T(8,128)(2,1)S(1)}, bf16[64,1024]{1,0:T(8,128)(2,1)S(1)}, u32[]{:S(2)}, u32[]{:S(2)}) collective-permute-start(bf16[64,1024]{1,0:T(8,128)(2,1)S(1)} %fusion.273), channel_id=1, source_target_pairs={{15,0},{0,1},{1,2},{2,3},{3,4},{4,5},{5,6},{6,7},{7,8},{8,9},{9,10... | collective-permute-start | bytes 393224 | tf_op jit(solution)/shard_map/ppermute | solution.py:13
  66.3 27.3 %collective-permute-start.4 = (bf16[64,1024]{1,0:T(8,128)(2,1)S(1)}, bf16[64,1024]{1,0:T(8,128)(2,1)S(1)}, u32[]{:S(2)}, u32[]{:S(2)}) collective-permute-start(bf16[64,1024]{1,0:T(8,128)(2,1)S(1)} %fusion.273), channel_id=1, source_target_pairs={{14,0},{15,1},{0,2},{1,3},{2,4},{3,5},{4,6},{5,7},{6,8},{7,9},{8,1... | collective-permute-start | bytes 393224 | tf_op jit(solution)/shard_map/ppermute | solution.py:13
  95.0 22.5 %collective-permute-start.8 = (bf16[2,64,1024]{2,1,0:T(8,128)(2,1)S(1)}, bf16[2,64,1024]{2,1,0:T(8,128)(2,1)S(1)}, u32[]{:S(2)}, u32[]{:S(2)}) collective-permute-start(bf16[2,64,1024]{2,1,0:T(8,128)(2,1)S(1)} %get-tuple-element.10), channel_id=1, source_target_pairs={{1,0},{2,1},{3,2},{4,3},{5,4},{6,5},{7,6},{8,7},{9,8},{10,9},{11,1... | collective-permute-start | bytes 786440 | tf_op jit(solution)/shard_map/ppermute | solution.py:13
  96.5 21.6 %collective-permute-start.10 = (bf16[2,64,1024]{2,1,0:T(8,128)(2,1)S(1)}, bf16[2,64,1024]{2,1,0:T(8,128)(2,1)S(1)}, u32[]{:S(2)}, u32[]{:S(2)}) collective-permute-start(bf16[2,64,1024]{2,1,0:T(8,128)(2,1)S(1)} %get-tuple-element.10), channel_id=1, source_target_pairs={{15,0},{0,1},{1,2},{2,3},{3,4},{4,5},{5,6},{6,7},{7,8},{8,9},{9,10... | collective-permute-start | bytes 786440 | tf_op jit(solution)/shard_map/ppermute | solution.py:13
  117.4 4.2 %collective-permute-start.9 = (bf16[2,64,1024]{2,1,0:T(8,128)(2,1)S(1)}, bf16[2,64,1024]{2,1,0:T(8,128)(2,1)S(1)}, u32[]{:S(2)}, u32[]{:S(2)}) collective-permute-start(bf16[2,64,1024]{2,1,0:T(8,128)(2,1)S(1)} %collective-permute-done.8), channel_id=1, source_target_pairs={{1,0},{2,1},{3,2},{4,3},{5,4},{6,5},{7,6},{8,7},{9,8},{10,9},{11,1... | collective-permute-start | bytes 786440 | tf_op jit(solution)/shard_map/ppermute | solution.py:13
  118.1 8.5 %collective-permute-start.11 = (bf16[2,64,1024]{2,1,0:T(8,128)(2,1)S(1)}, bf16[2,64,1024]{2,1,0:T(8,128)(2,1)S(1)}, u32[]{:S(2)}, u32[]{:S(2)}) collective-permute-start(bf16[2,64,1024]{2,1,0:T(8,128)(2,1)S(1)} %collective-permute-done.10), channel_id=1, source_target_pairs={{15,0},{0,1},{1,2},{2,3},{3,4},{4,5},{5,6},{6,7},{7,8},{8,9},{9,10... | collective-permute-start | bytes 786440 | tf_op jit(solution)/shard_map/ppermute | solution.py:13
  128.2 29.0 %collective-permute-start.15 = (bf16[64,1024]{1,0:T(8,128)(2,1)S(1)}, bf16[64,1024]{1,0:T(8,128)(2,1)S(1)}, u32[]{:S(2)}, u32[]{:S(2)}) collective-permute-start(bf16[64,1024]{1,0:T(8,128)(2,1)S(1)} %fusion.276), channel_id=1, source_target_pairs={{2,0},{3,1},{4,2},{5,3},{6,4},{7,5},{8,6},{9,7},{10,8},{11,9},{12,... | collective-permute-start | bytes 393224 | tf_op jit(solution)/shard_map/ppermute | solution.py:13
  128.9 27.4 %collective-permute-start.14 = (bf16[64,1024]{1,0:T(8,128)(2,1)S(1)}, bf16[64,1024]{1,0:T(8,128)(2,1)S(1)}, u32[]{:S(2)}, u32[]{:S(2)}) collective-permute-start(bf16[64,1024]{1,0:T(8,128)(2,1)S(1)} %fusion.276), channel_id=1, source_target_pairs={{1,0},{2,1},{3,2},{4,3},{5,4},{6,5},{7,6},{8,7},{9,8},{10,9},{11,1... | collective-permute-start | bytes 393224 | tf_op jit(solution)/shard_map/ppermute | solution.py:13
  130.7 24.7 %collective-permute-start.13 = (bf16[64,1024]{1,0:T(8,128)(2,1)S(1)}, bf16[64,1024]{1,0:T(8,128)(2,1)S(1)}, u32[]{:S(2)}, u32[]{:S(2)}) collective-permute-start(bf16[64,1024]{1,0:T(8,128)(2,1)S(1)} %fusion.276), channel_id=1, source_target_pairs={{15,0},{0,1},{1,2},{2,3},{3,4},{4,5},{5,6},{6,7},{7,8},{8,9},{9,10... | collective-permute-start | bytes 393224 | tf_op jit(solution)/shard_map/ppermute | solution.py:13
  130.8 27.2 %collective-permute-start.12 = (bf16[64,1024]{1,0:T(8,128)(2,1)S(1)}, bf16[64,1024]{1,0:T(8,128)(2,1)S(1)}, u32[]{:S(2)}, u32[]{:S(2)}) collective-permute-start(bf16[64,1024]{1,0:T(8,128)(2,1)S(1)} %fusion.276), channel_id=1, source_target_pairs={{14,0},{15,1},{0,2},{1,3},{2,4},{3,5},{4,6},{5,7},{6,8},{7,9},{8,1... | collective-permute-start | bytes 393224 | tf_op jit(solution)/shard_map/ppermute | solution.py:13
  159.3 22.5 %collective-permute-start.16 = (bf16[2,64,1024]{2,1,0:T(8,128)(2,1)S(1)}, bf16[2,64,1024]{2,1,0:T(8,128)(2,1)S(1)}, u32[]{:S(2)}, u32[]{:S(2)}) collective-permute-start(bf16[2,64,1024]{2,1,0:T(8,128)(2,1)S(1)} %get-tuple-element.12), channel_id=1, source_target_pairs={{1,0},{2,1},{3,2},{4,3},{5,4},{6,5},{7,6},{8,7},{9,8},{10,9},{11,1... | collective-permute-start | bytes 786440 | tf_op jit(solution)/shard_map/ppermute | solution.py:13
  160.7 21.9 %collective-permute-start.18 = (bf16[2,64,1024]{2,1,0:T(8,128)(2,1)S(1)}, bf16[2,64,1024]{2,1,0:T(8,128)(2,1)S(1)}, u32[]{:S(2)}, u32[]{:S(2)}) collective-permute-start(bf16[2,64,1024]{2,1,0:T(8,128)(2,1)S(1)} %get-tuple-element.12), channel_id=1, source_target_pairs={{15,0},{0,1},{1,2},{2,3},{3,4},{4,5},{5,6},{6,7},{7,8},{8,9},{9,10... | collective-permute-start | bytes 786440 | tf_op jit(solution)/shard_map/ppermute | solution.py:13
  181.8 4.4 %collective-permute-start.17 = (bf16[2,64,1024]{2,1,0:T(8,128)(2,1)S(1)}, bf16[2,64,1024]{2,1,0:T(8,128)(2,1)S(1)}, u32[]{:S(2)}, u32[]{:S(2)}) collective-permute-start(bf16[2,64,1024]{2,1,0:T(8,128)(2,1)S(1)} %collective-permute-done.16), channel_id=1, source_target_pairs={{1,0},{2,1},{3,2},{4,3},{5,4},{6,5},{7,6},{8,7},{9,8},{10,9},{11,1... | collective-permute-start | bytes 786440 | tf_op jit(solution)/shard_map/ppermute | solution.py:13
  182.6 8.5 %collective-permute-start.19 = (bf16[2,64,1024]{2,1,0:T(8,128)(2,1)S(1)}, bf16[2,64,1024]{2,1,0:T(8,128)(2,1)S(1)}, u32[]{:S(2)}, u32[]{:S(2)}) collective-permute-start(bf16[2,64,1024]{2,1,0:T(8,128)(2,1)S(1)} %collective-permute-done.18), channel_id=1, source_target_pairs={{15,0},{0,1},{1,2},{2,3},{3,4},{4,5},{5,6},{6,7},{7,8},{8,9},{9,10... | collective-permute-start | bytes 786440 | tf_op jit(solution)/shard_map/ppermute | solution.py:13
  193.4 29.0 %collective-permute-start.23 = (bf16[64,1024]{1,0:T(8,128)(2,1)S(1)}, bf16[64,1024]{1,0:T(8,128)(2,1)S(1)}, u32[]{:S(2)}, u32[]{:S(2)}) collective-permute-start(bf16[64,1024]{1,0:T(8,128)(2,1)S(1)} %get-tuple-element.14), channel_id=1, source_target_pairs={{2,0},{3,1},{4,2},{5,3},{6,4},{7,5},{8,6},{9,7},{10,8},{11,9},{12,... | collective-permute-start | bytes 393224 | tf_op jit(solution)/shard_map/ppermute | solution.py:13
  194.2 27.4 %collective-permute-start.22 = (bf16[64,1024]{1,0:T(8,128)(2,1)S(1)}, bf16[64,1024]{1,0:T(8,128)(2,1)S(1)}, u32[]{:S(2)}, u32[]{:S(2)}) collective-permute-start(bf16[64,1024]{1,0:T(8,128)(2,1)S(1)} %get-tuple-element.14), channel_id=1, source_target_pairs={{1,0},{2,1},{3,2},{4,3},{5,4},{6,5},{7,6},{8,7},{9,8},{10,9},{11,1... | collective-permute-start | bytes 393224 | tf_op jit(solution)/shard_map/ppermute | solution.py:13
  196.0 24.7 %collective-permute-start.21 = (bf16[64,1024]{1,0:T(8,128)(2,1)S(1)}, bf16[64,1024]{1,0:T(8,128)(2,1)S(1)}, u32[]{:S(2)}, u32[]{:S(2)}) collective-permute-start(bf16[64,1024]{1,0:T(8,128)(2,1)S(1)} %get-tuple-element.14), channel_id=1, source_target_pairs={{15,0},{0,1},{1,2},{2,3},{3,4},{4,5},{5,6},{6,7},{7,8},{8,9},{9,10... | collective-permute-start | bytes 393224 | tf_op jit(solution)/shard_map/ppermute | solution.py:13
  196.0 27.2 %collective-permute-start.20 = (bf16[64,1024]{1,0:T(8,128)(2,1)S(1)}, bf16[64,1024]{1,0:T(8,128)(2,1)S(1)}, u32[]{:S(2)}, u32[]{:S(2)}) collective-permute-start(bf16[64,1024]{1,0:T(8,128)(2,1)S(1)} %get-tuple-element.14), channel_id=1, source_target_pairs={{14,0},{15,1},{0,2},{1,3},{2,4},{3,5},{4,6},{5,7},{6,8},{7,9},{8,1... | collective-permute-start | bytes 393224 | tf_op jit(solution)/shard_map/ppermute | solution.py:13
  (6 other events, 310.9 us)
where the time goes:
time: 226 us; the launch traced here: 225 us
  blocking collectives  121 us (54%)
  matrix products  57.3 us (25%)
  starting transfers between devices  23.4 us (10%)
  between operations  11 us (5%)
  waiting for transfers between devices  8.46 us (4%)
    all_gather x3, blocking collectives, on_device(): lax.all_gather(data_summary[None], 'row', axis=0, tiled=True)  63.2 us
    all_gather x3, blocking collectives, on_device(): add_received = lax.all_gather(summary[None], 'row', axis=0, tiled=True)  58.2 us
    dot_general x15, matrix products, on_device(): jnp.einsum('lpc,lac->pa', received_map[shift_by], tile_list[offset_slot],...  33.9 us
    ppermute x24, starting transfers between devices, shifted(): return lax.ppermute(block, axis, route)  23.4 us
    dot_general x15, matrix products, on_device(): jnp.einsum('pa,lac->lpc', received, tile_list[offset_slot], preferred_ele...  14.2 us
    ppermute x24, waiting for transfers between devices, shifted(): return lax.ppermute(block, axis, route)  8.46 us
  transfers between devices with their start and end apart: 24, of which 4 were waited for; matrix products, arithmetic and copies ran while one was open for 22% of the time, Pallas kernels for 0%

commit v1 on v0

v1 whole, which is shorter than its diff:
```python
import functools

import jax
import jax.numpy as jnp
from jax import lax
from jax.experimental import pallas as pl
from jax.experimental.pallas import tpu as pltpu
from jax.sharding import PartitionSpec as P

RADIUS = 2
ITERS = 3
SPAN = 2 * RADIUS + 1
STEP = 0.01
DAMPING = 10.0
COPIES = 3
LANES = 128
STRIP = 256
CHUNK = 512


def dot(left, right):
    return lax.dot_general(
        left, right, (((1,), (0,)), ((), ())), preferred_element_type=jnp.float32
    )


def dot_full(left, right):
    return lax.dot_general(
        left,
        right,
        (((1,), (0,)), ((), ())),
        precision=lax.Precision.HIGHEST,
        preferred_element_type=jnp.float32,
    )


def tables_kernel(
    source_ref,
    receiver_ref,
    ahead_ref,
    back_ref,
    source_wide,
    receiver_wide,
    core_ahead,
    core_back,
    receiver_rows,
    source_rows,
):
    layers, rank = source_ref.shape[:2]
    receiver_rows[...] = jnp.zeros_like(receiver_rows)
    source_rows[...] = jnp.zeros_like(source_rows)
    for l in range(layers):
        for c in range(COPIES):
            first = (l * COPIES + c) * rank
            receiver_rows[first : first + rank, :] = receiver_ref[l]
            source_rows[l, first : first + rank, :] = source_ref[l]
        source_wide[l] = jnp.concatenate([source_ref[l]] * (LANES // rank), 0).T
        receiver_wide[l] = jnp.concatenate([receiver_ref[l]] * (LANES // rank), 0).T
        before, after = l * COPIES * rank, LANES - (l + 1) * COPIES * rank
        for narrow, out in ((ahead_ref, core_ahead), (back_ref, core_back)):
            block = narrow[l]
            parts = [block] * COPIES
            if before:
                parts = [jnp.zeros((block.shape[0], before), jnp.float32)] + parts
            parts = parts + [jnp.zeros((block.shape[0], after), jnp.float32)]
            out[l] = jnp.concatenate(parts, 1)


def pack_rows(packed, bands, layers, own, cells, block_of, data_of):
    stride = layers * own
    share = cells // layers
    for l in range(layers):
        for p in range(own):
            block = block_of(l, p)
            data = data_of(p)
            for j in range(cells // LANES):
                packed[j, pl.ds(l * own + p, bands, stride=stride), :] = block[
                    :, j * LANES : (j + 1) * LANES
                ]
            for j in range(share // LANES):
                start = l * share + j * LANES
                packed[cells // LANES + j, pl.ds(l * own + p, bands, stride=stride), :] = data[
                    :, start : start + LANES
                ]


def flush(packed, out_ref):
    for j in range(packed.shape[0]):
        out_ref[:, j * LANES : (j + 1) * LANES] = packed[j].astype(out_ref.dtype)


def fetch(in_ref, packed):
    for j in range(packed.shape[0]):
        packed[j] = in_ref[:, j * LANES : (j + 1) * LANES].astype(jnp.float32)


def unpack_rows(packed, bands, layers, own, cells, store_model, store_data):
    stride = layers * own
    share = cells // layers
    for l in range(layers):
        for p in range(own):
            rows = pl.ds(l * own + p, bands, stride=stride)
            for j in range(cells // LANES):
                store_model(l, p, j * LANES, packed[j, rows, :])
            for j in range(share // LANES):
                store_data(p, l * share + j * LANES, packed[cells // LANES + j, rows, :])


def pack_kernel(model_ref, data_ref, out_ref, packed, *, bands, own):
    layers, perts, cells = model_ref.shape

    def rows_of(values, p):
        held = min(bands, perts - p * bands)
        block = values[p * bands : p * bands + held, :].astype(jnp.float32)
        if held < bands:
            block = jnp.concatenate([block, jnp.zeros((bands - held, cells), jnp.float32)], 0)
        return block

    pack_rows(
        packed,
        bands,
        layers,
        own,
        cells,
        lambda l, p: rows_of(model_ref.at[l], p),
        lambda p: rows_of(data_ref, p),
    )
    flush(packed, out_ref)


def unpack_kernel(in_ref, model_ref, data_ref, packed, *, bands, own):
    layers, perts, cells = model_ref.shape
    fetch(in_ref, packed)

    def store_model(l, p, lane, block):
        held = min(bands, perts - p * bands)
        model_ref[l, p * bands : p * bands + held, lane : lane + LANES] = block[:held]

    def store_data(p, lane, block):
        held = min(bands, perts - p * bands)
        data_ref[p * bands : p * bands + held, lane : lane + LANES] = block[:held]

    unpack_rows(packed, bands, layers, own, cells, store_model, store_data)


def rolled(values, shift, bands, own):
    shift = shift % bands
    if shift == 0:
        return values
    return jnp.concatenate(
        [pltpu.roll(values[p * bands : (p + 1) * bands], shift, 0) for p in range(own)], 0
    )


def staircase(values, sign, rank, bands, own):
    group = lax.broadcasted_iota(jnp.int32, values.shape, 1) // rank
    bit = 1
    while bit < LANES // rank:
        values = jnp.where((group & bit) != 0, rolled(values, sign * bit, bands, own), values)
        bit *= 2
    return values


def split_parts(values, rank):
    part = (lax.broadcasted_iota(jnp.int32, values.shape, 1) // rank) % COPIES
    high = values.astype(jnp.bfloat16).astype(jnp.float32)
    rest = values - high
    middle = rest.astype(jnp.bfloat16).astype(jnp.float32)
    low = rest - middle
    return jnp.where(part == 0, high, jnp.where(part == 1, middle, low)).astype(jnp.bfloat16)


def steps_kernel(
    order_ref,
    packed_in,
    tiles_hbm,
    source_wide,
    receiver_wide,
    core_ahead,
    core_back,
    receiver_rows,
    source_rows,
    packed_out,
    packed,
    model,
    measured,
    misfit,
    wire,
    tiles,
    flipped,
    sems,
    *,
    bands,
    own,
    rank,
):
    layers, span = tiles.shape[:2]
    cells = tiles.shape[3]

    def copy(j):
        part = pl.ds(j * STRIP, STRIP)
        return pltpu.make_async_copy(
            tiles_hbm.at[:, :, part, :], tiles.at[:, :, part, :], sems.at[j]
        )

    for j in range(cells // STRIP):
        copy(j).start()
    fetch(packed_in, packed)

    def store_model(l, p, lane, block):
        model[l, p * bands : (p + 1) * bands, lane : lane + LANES] = block

    def store_data(p, lane, block):
        measured[p * bands : (p + 1) * bands, lane : lane + LANES] = block

    unpack_rows(packed, bands, layers, own, cells, store_model, store_data)

    sent = wire.at[0]
    slots = []
    for offset in range(span):
        slot = jnp.int32(0)
        for k in range(1, span):
            slot = slot + jnp.where(order_ref[k] == offset, k, 0)
        slots.append(slot)
    groups = bands // (LANES // rank)

    def far(wide, cores, sign):
        total = jnp.zeros((bands * own, LANES), jnp.float32)
        for l in range(layers):
            stair = staircase(wide[l], sign, rank, bands, own)

            def add(g, carry, l=l):
                moved, total = carry
                start = pl.multiple_of(g * LANES, LANES)
                total = total + dot_full(moved, cores[l, pl.ds(start, LANES), :])
                return rolled(moved, sign * (LANES // rank), bands, own), total

            total = lax.fori_loop(0, groups, add, (stair, total), unroll=groups <= 2)[1]
        return split_parts(total, rank)

    def step(first):
        wide = []
        for l in range(layers):
            value = model[l]
            for offset in range(span):
                wire[l, slots[offset]] = rolled(value, offset - RADIUS, bands, own).astype(
                    jnp.bfloat16
                )
            wide.append(dot(value.astype(jnp.bfloat16), source_wide[l]))
        field = far(wide, core_ahead, 1)
        for j in range(cells // STRIP):
            part = slice(j * STRIP, (j + 1) * STRIP)
            if first:
                copy(j).wait()
            predicted = dot(field, receiver_rows[:, part])
            for l in range(layers):
                for k in range(span):
                    if first:
                        block = tiles[l, k, part, :].T
                        flipped[l, k, :, part] = block
                    else:
                        block = flipped[l, k, :, part]
                    predicted = predicted + dot(wire[l, k], block)
            misfit[:, part] = measured[:, part] - predicted
        residual = misfit[...]
        for offset in range(span):
            sent[slots[offset]] = rolled(residual, RADIUS - offset, bands, own).astype(
                jnp.bfloat16
            )
        rounded = residual.astype(jnp.bfloat16)
        back = far([dot(rounded, receiver_wide[l]) for l in range(layers)], core_back, -1)
        for l in range(layers):
            for j in range(cells // CHUNK):
                part = slice(j * CHUNK, (j + 1) * CHUNK)
                gradient = dot(back, source_rows[l, :, part])
                for k in range(span):
                    gradient = gradient + dot(sent[k], tiles[l, k, :, part])
                value = model[l, :, part]
                model[l, :, part] = value + STEP * (gradient - DAMPING * value)

    step(True)
    lax.fori_loop(1, ITERS, lambda index, carry: (step(False), carry)[1], 0)
    pack_rows(
        packed,
        bands,
        layers,
        own,
        cells,
        lambda l, p: model[l, p * bands : (p + 1) * bands, :],
        lambda p: misfit[p * bands : (p + 1) * bands, :],
    )
    flush(packed, packed_out)


def whole_array():
    return pl.BlockSpec(memory_space=pltpu.VMEM)


def on_device(
    near_tiles, near_order, receiver_basis, source_basis, coupling, initial_model, observed, *, bands
):
    layers, perts, cells = initial_model.shape
    rank = coupling.shape[-1]
    own = -(-perts // bands)
    held = layers * own
    rows = bands * held
    width = cells + cells // layers
    cols = bands * own
    bf16, f32 = jnp.bfloat16, jnp.float32

    packed = pl.pallas_call(
        functools.partial(pack_kernel, bands=bands, own=own),
        out_shape=jax.ShapeDtypeStruct((rows, width), bf16),
        in_specs=[whole_array()] * 2,
        out_specs=whole_array(),
        scratch_shapes=[pltpu.VMEM((width // LANES, rows, LANES), f32)],
        name="pack",
    )(initial_model, observed)
    received = lax.all_to_all(packed.reshape(bands, held, width), "row", 0, 0, tiled=True)

    span = near_tiles.shape[1]
    tables = pl.pallas_call(
        tables_kernel,
        out_shape=[
            jax.ShapeDtypeStruct((layers, cells, LANES), bf16),
            jax.ShapeDtypeStruct((layers, cells, LANES), bf16),
            jax.ShapeDtypeStruct((layers, bands * rank, LANES), f32),
            jax.ShapeDtypeStruct((layers, bands * rank, LANES), f32),
            jax.ShapeDtypeStruct((LANES, cells), bf16),
            jax.ShapeDtypeStruct((layers, LANES, cells), bf16),
        ],
        in_specs=[whole_array()] * 4,
        out_specs=[whole_array()] * 6,
        name="tables",
    )(
        source_basis.transpose(0, 2, 1),
        receiver_basis.transpose(0, 2, 1),
        coupling.transpose(0, 1, 3, 2).reshape(layers, bands * rank, rank),
        coupling.reshape(layers, bands * rank, rank),
    )

    result = pl.pallas_call(
        functools.partial(steps_kernel, bands=bands, own=own, rank=rank),
        out_shape=jax.ShapeDtypeStruct((rows, width), bf16),
        in_specs=[
            pl.BlockSpec(memory_space=pltpu.SMEM),
            whole_array(),
            pl.BlockSpec(memory_space=pl.ANY),
        ]
        + [whole_array()] * 6,
        out_specs=whole_array(),
        scratch_shapes=[
            pltpu.VMEM((width // LANES, rows, LANES), f32),
            pltpu.VMEM((layers, cols, cells), f32),
            pltpu.VMEM((cols, cells), f32),
            pltpu.VMEM((cols, cells), f32),
            pltpu.VMEM((layers, span, cols, cells), bf16),
            pltpu.VMEM(near_tiles.shape, bf16),
            pltpu.VMEM(near_tiles.shape, bf16),
            pltpu.SemaphoreType.DMA((cells // STRIP,)),
        ],
        compiler_params=pltpu.CompilerParams(vmem_limit_bytes=60 << 20),
        name="steps",
    )(
        near_order,
        received.reshape(rows, width),
        near_tiles,
        *tables,
    )
    returned = lax.all_to_all(result.reshape(bands, held, width), "row", 0, 0, tiled=True)
    return pl.pallas_call(
        functools.partial(unpack_kernel, bands=bands, own=own),
        out_shape=(
            jax.ShapeDtypeStruct((layers, perts, cells), f32),
            jax.ShapeDtypeStruct((perts, cells), f32),
        ),
        in_specs=[whole_array()],
        out_specs=(whole_array(), whole_array()),
        scratch_shapes=[pltpu.VMEM((width // LANES, rows, LANES), f32)],
        name="unpack",
    )(returned.reshape(rows, width))


def solution(mesh):
    placed = (P(), P(), P(), P(), P(), P(None, "group", "row"), P("group", "row"))
    return jax.shard_map(
        functools.partial(on_device, bands=mesh.shape["row"]),
        mesh=mesh,
        in_specs=placed,
        out_specs=(P(None, "group", "row"), P("group", "row")),
        check_vma=False,
    )
```

time: 226 us -> 76.2 us (0.34)
  blocking collectives: 121 us -> 16.4 us
  matrix products: 57.3 us -> 0 us
  Pallas kernels: 0 us -> 41.2 us
  starting transfers between devices: 23.4 us -> 7.41 us
  between operations: 11 us -> 0.65 us
    all_gather x6 -> x0, blocking collectives: 121 us -> none  [the longest x3 63.2 us: on_device(): lax.all_gather(data_summary[None], 'row', axis=0, tiled=True)]
    dot_general x45 -> x0, matrix products: 56.9 us -> none  [the longest x15 33.9 us: on_device(): jnp.einsum('lpc,lac->pa', received_map[shift_by], tile_list[offset_slot],...]
    pallas_call x0 -> x4, Pallas kernels: none -> 41.2 us  [the longest x1 34.3 us: on_device(): pl.pallas_call(functools.partial(steps_kernel, bands=bands, own=own, rank...]
    ppermute x24 -> x0, starting transfers between devices: 23.4 us -> none  [shifted(): return lax.ppermute(block, axis, route)]
    all_to_all x0 -> x1, blocking collectives: none -> 16.4 us  [on_device(): lax.all_to_all(result.reshape(bands, held, width), 'row', 0, 0, tiled=True)]
    ppermute x24 -> x0, waiting for transfers between devices: 8.46 us -> none  [shifted(): return lax.ppermute(block, axis, route)]
    all_to_all x0 -> x1, waiting for transfers between devices: none -> 7.55 us  [on_device(): lax.all_to_all(packed.reshape(bands, held, width), 'row', 0, 0, tiled=True)]
    all_to_all x0 -> x1, starting transfers between devices: none -> 7.41 us  [on_device(): lax.all_to_all(packed.reshape(bands, held, width), 'row', 0, 0, tiled=True)]
  transfers between devices with their start and end apart: 24 -> 1, of which waited for: 4 -> 1; matrix products, arithmetic and copies ran while one was open for 22% -> 2% of each run, Pallas kernels for 0% -> 4%
where the time goes in v1:
time: 76.2 us; the launch traced here: 75.7 us
  Pallas kernels  41.2 us (54%)
  blocking collectives  16.4 us (22%)
  waiting for transfers between devices  7.55 us (10%)
  starting transfers between devices  7.41 us (10%)
  local copies, waits for them, and re-layouts  2.53 us (3%)
    pallas_call x1, Pallas kernels, on_device(): pl.pallas_call(functools.partial(steps_kernel, bands=bands, own=own, rank...  34.3 us
    all_to_all x1, blocking collectives, on_device(): lax.all_to_all(result.reshape(bands, held, width), 'row', 0, 0, tiled=True)  16.4 us
    all_to_all x1, waiting for transfers between devices, on_device(): lax.all_to_all(packed.reshape(bands, held, width), 'row', 0, 0, tiled=True)  7.55 us
    all_to_all x1, starting transfers between devices, on_device(): lax.all_to_all(packed.reshape(bands, held, width), 'row', 0, 0, tiled=True)  7.41 us
    pallas_call x1, Pallas kernels, on_device(): pl.pallas_call(tables_kernel, out_shape=[jax.ShapeDtypeStruct((layers, ce...  2.82 us
    pallas_call x1, Pallas kernels, on_device(): pl.pallas_call(functools.partial(unpack_kernel, bands=bands, own=own), ou...  2.05 us
    pallas_call x1, Pallas kernels, on_device(): pl.pallas_call(functools.partial(pack_kernel, bands=bands, own=own), out_...  1.99 us
    transpose x1, local copies, waits for them, and re-layouts, on_device(): coupling.transpose(0, 1, 3, 2).reshape(layers, bands * rank, rank)  1.79 us
  transfers between devices with their start and end apart: 1, of which 1 were waited for; matrix products, arithmetic and copies ran while one was open for 2% of the time, Pallas kernels for 4%

profile of v1, /device:TPU:0, one launch (start us, length us, event | category | flops | bytes accessed | tf_op | source)
XLA Modules:
  0.0 75.7 jit_solution(10269992653060706828)
XLA Ops:
  0.6 2.0 %pack.1 = bf16[128,1536]{1,0:T(8,128)(2,1)} custom-call(bf16[2,64,1024]{2,1,0:T(8,128)(2,1)} %model_ref.1, bf16[64,1024]{1,0:T(8,128)(2,1)} %data_ref.1), custom_call_target="tpu_custom_call" | custom-call | tf_op jit(solution)/shard_map/pack/pallas_call | solution.py:311
  2.6 7.4 %all-to-all-start = ((bf16[16,8,1536]{2,1,0:T(8,128)(2,1)}), bf16[16,8,1536]{2,1,0:T(8,128)(2,1)S(1)}, u32[]{:S(2)}, u32[]{:S(2)}) async-start(bf16[16,8,1536]{2,1,0:T(8,128)(2,1)} %bitcast.9), calls=%async_computation | async-start | bytes 786432 | tf_op jit(solution)/shard_map/all_to_all | solution.py:319
  10.0 1.8 %copy.9 = f32[2,16,16,16]{3,2,1,0:T(8,128)} copy(f32[2,16,16,16]{2,3,1,0:T(8,128)} %bitcast.13) | data formatting | bytes 65536 | tf_op jit(solution)/shard_map/transpose | solution.py:338
  11.8 2.8 %tables.1 = (bf16[2,1024,128]{2,1,0:T(8,128)(2,1)}, bf16[2,1024,128]{2,1,0:T(8,128)(2,1)}, f32[2,256,128]{2,1,0:T(8,128)}, f32[2,256,128]{2,1,0:T(8,128)}, bf16[...) custom-call(bf16[2,16,1024]{2,1,0:T(8,128)(2,1)} %bitcast.16, bf16[2,16,1024]{2,1,0:T(8,128)(2,1)} %bitcast.17, ...), custom_call_target="tpu_custom_call" | custom-call | tf_op jit(solution)/shard_map/tables/pallas_call | solution.py:322
  14.7 7.6 %all-to-all-done = bf16[16,8,1536]{2,1,0:T(8,128)(2,1)S(1)} async-done(((bf16[16,8,1536]{2,1,0:T(8,128)(2,1)}), bf16[16,8,1536]{2,1,0:T(8,128)(2,1)S(1)}, u32[]{:S(2)}, u32[]{:S(2)}) %all-to-all-start) | async-done | bytes 393248 | tf_op jit(solution)/shard_map/all_to_all | solution.py:319
  22.2 0.0 copy-start
  22.2 0.7 copy-done
  23.0 34.3 %steps.1 = bf16[128,1536]{1,0:T(8,128)(2,1)} custom-call(s32[5]{0:T(128)} %order_ref.1, bf16[128,1536]{1,0:T(8,128)(2,1)} %bitcast.11, bf16[2,5,1024,1024]{3,2,1,0:T(8,128)(2,1)} %tiles_hbm.1, bf16[2,1024,128]{2,1,0:T(8,128)(2,1)} %get-tuple-element.8.source_wide, bf16[2,1024,128]{2,1,0:T(8,128)(2,1)} %get-tuple-element.9.receiver_wide, ...), custom_call_target="tpu_custom_call" | custom-call | tf_op jit(solution)/shard_map/steps/pallas_call | solution.py:342
  57.3 16.4 %all_to_all.10 = bf16[16,8,1536]{2,1,0:T(8,128)(2,1)} all-to-all(bf16[16,8,1536]{2,1,0:T(8,128)(2,1)} %bitcast.12), channel_id=1, replica_groups=mesh['group'=2,'row'=16] {'row'}, dimensions={0} | all-to-all | bytes 786432 | tf_op jit(solution)/shard_map/all_to_all | solution.py:370
  73.7 2.0 %unpack.1 = (f32[2,64,1024]{2,1,0:T(8,128)}, f32[64,1024]{1,0:T(8,128)}) custom-call(bf16[128,1536]{1,0:T(8,128)(2,1)} %bitcast.10), custom_call_target="tpu_custom_call" | custom-call | tf_op jit(solution)/shard_map/unpack/pallas_call | solution.py:371
Async XLA Ops:
  2.6 19.6 %all-to-all-start = ((bf16[16,8,1536]{2,1,0:T(8,128)(2,1)}), bf16[16,8,1536]{2,1,0:T(8,128)(2,1)S(1)}, u32[]{:S(2)}, u32[]{:S(2)}) async-start(bf16[16,8,1536]{2,1,0:T(8,128)(2,1)} %bitcast.9), calls=%async_computation | async-start | bytes 786432 | tf_op jit(solution)/shard_map/all_to_all | solution.py:319
  22.2 0.7 copy-start

commit v2 on v1

v2 whole, which is shorter than its diff:
```python
import functools

import jax
import jax.numpy as jnp
from jax import lax
from jax.experimental import pallas as pl
from jax.experimental.pallas import tpu as pltpu
from jax.sharding import PartitionSpec as P

RADIUS = 2
ITERS = 3
SPAN = 2 * RADIUS + 1
STEP = 0.01
DAMPING = 10.0
COPIES = 3
LANES = 128
STRIP = 256
CHUNK = 512
SMALL = 8 << 20


def dot(left, right):
    return lax.dot_general(
        left, right, (((1,), (0,)), ((), ())), preferred_element_type=jnp.float32
    )


def dot_full(left, right):
    return lax.dot_general(
        left,
        right,
        (((1,), (0,)), ((), ())),
        precision=lax.Precision.HIGHEST,
        preferred_element_type=jnp.float32,
    )


def tables_kernel(
    source_ref,
    receiver_ref,
    ahead_ref,
    back_ref,
    source_wide,
    receiver_wide,
    core_ahead,
    core_back,
    receiver_rows,
    source_rows,
):
    layers, rank = source_ref.shape[:2]
    receiver_rows[...] = jnp.zeros_like(receiver_rows)
    source_rows[...] = jnp.zeros_like(source_rows)
    for l in range(layers):
        for c in range(COPIES):
            first = (l * COPIES + c) * rank
            receiver_rows[first : first + rank, :] = receiver_ref[l]
            source_rows[l, first : first + rank, :] = source_ref[l]
        source_wide[l] = jnp.concatenate([source_ref[l]] * (LANES // rank), 0).T
        receiver_wide[l] = jnp.concatenate([receiver_ref[l]] * (LANES // rank), 0).T
        before, after = l * COPIES * rank, LANES - (l + 1) * COPIES * rank
        for narrow, out in ((ahead_ref, core_ahead), (back_ref, core_back)):
            block = narrow[l]
            parts = [block] * COPIES
            if before:
                parts = [jnp.zeros((block.shape[0], before), jnp.float32)] + parts
            parts = parts + [jnp.zeros((block.shape[0], after), jnp.float32)]
            out[l] = jnp.concatenate(parts, 1)


def exchanged(first, second, own):
    shape = first.shape
    first = first.reshape(-1, 2 * own, shape[-1])
    second = second.reshape(-1, 2 * own, shape[-1])
    low = lax.broadcasted_iota(jnp.int32, first.shape, 1) < own
    even = jnp.where(low, first, pltpu.roll(second, own, 1))
    odd = jnp.where(low, pltpu.roll(first, own, 1), second)
    return even, odd


def merged(first, second, own):
    even, odd = exchanged(first, second, own)
    return jnp.stack([even, odd], 1).reshape(-1, first.shape[-1])


def parted(values, own):
    pairs = values.reshape(-1, 2, 2 * own, values.shape[-1])
    low = lax.broadcasted_iota(jnp.int32, pairs[:, 0].shape, 1) < own
    even, odd = pairs[:, 0], pairs[:, 1]
    first = jnp.where(low, even, pltpu.roll(odd, own, 1))
    second = jnp.where(low, pltpu.roll(even, own, 1), odd)
    return first.reshape(-1, values.shape[-1]), second.reshape(-1, values.shape[-1])


def pack_kernel(model_ref, data_ref, out_ref, *, own):
    cells = model_ref.shape[-1]
    half = cells // 2
    f32 = jnp.float32
    out_ref[:, :cells] = merged(
        model_ref[0].astype(f32), model_ref[1].astype(f32), own
    ).astype(out_ref.dtype)
    out_ref[:, cells:] = merged(
        data_ref[:, :half].astype(f32), data_ref[:, half:].astype(f32), own
    ).astype(out_ref.dtype)


def unpack_kernel(in_ref, model_ref, data_ref, *, own):
    cells = model_ref.shape[-1]
    half = cells // 2
    model_ref[0], model_ref[1] = parted(in_ref[:, :cells].astype(jnp.float32), own)
    data_ref[:, :half], data_ref[:, half:] = parted(
        in_ref[:, cells:].astype(jnp.float32), own
    )


def rolled(values, shift, own):
    shift = (shift * own) % values.shape[0]
    return pltpu.roll(values, shift, 0) if shift else values


def staircase(values, sign, rank, own):
    group = lax.broadcasted_iota(jnp.int32, values.shape, 1) // rank
    bit = 1
    while bit < LANES // rank:
        values = jnp.where((group & bit) != 0, rolled(values, sign * bit, own), values)
        bit *= 2
    return values


def split_parts(values, rank):
    part = (lax.broadcasted_iota(jnp.int32, values.shape, 1) // rank) % COPIES
    high = values.astype(jnp.bfloat16).astype(jnp.float32)
    rest = values - high
    middle = rest.astype(jnp.bfloat16).astype(jnp.float32)
    low = rest - middle
    return jnp.where(part == 0, high, jnp.where(part == 1, middle, low)).astype(jnp.bfloat16)


def steps_kernel(
    order_ref,
    packed_in,
    tiles_hbm,
    source_wide,
    receiver_wide,
    core_ahead,
    core_back,
    receiver_rows,
    source_rows,
    packed_out,
    model,
    measured,
    misfit,
    wire,
    tiles,
    flipped,
    sems,
    *,
    bands,
    own,
    rank,
    paired,
):
    layers, span = tiles.shape[:2]
    cells = tiles.shape[3]
    share = cells // layers
    cols = bands * own

    def copy(j):
        part = pl.ds(j * STRIP, STRIP)
        return pltpu.make_async_copy(
            tiles_hbm.at[:, :, part, :], tiles.at[:, :, part, :], sems.at[j]
        )

    for j in range(cells // STRIP):
        copy(j).start()
    if paired:
        model[0], model[1] = parted(packed_in[:, :cells].astype(jnp.float32), own)
        measured[:, :share], measured[:, share:] = parted(
            packed_in[:, cells:].astype(jnp.float32), own
        )
    else:
        for l in range(layers):
            rows = slice(l * cols, (l + 1) * cols)
            model[l] = packed_in[rows, :cells].astype(jnp.float32)
            measured[:, l * share : (l + 1) * share] = packed_in[rows, cells:].astype(jnp.float32)

    sent = wire.at[0]
    slots = []
    for offset in range(span):
        slot = jnp.int32(0)
        for k in range(1, span):
            slot = slot + jnp.where(order_ref[k] == offset, k, 0)
        slots.append(slot)
    groups = bands // (LANES // rank)

    def far(wide, cores, sign):
        total = jnp.zeros((cols, LANES), jnp.float32)
        for l in range(layers):
            stair = staircase(wide[l], sign, rank, own)

            def add(g, carry, l=l):
                moved, total = carry
                start = pl.multiple_of(g * LANES, LANES)
                total = total + dot_full(moved, cores[l, pl.ds(start, LANES), :])
                return rolled(moved, sign * (LANES // rank), own), total

            total = lax.fori_loop(0, groups, add, (stair, total), unroll=groups <= 2)[1]
        return split_parts(total, rank)

    def step(first):
        wide = []
        for l in range(layers):
            value = model[l]
            for offset in range(span):
                wire[l, slots[offset]] = rolled(value, offset - RADIUS, own).astype(jnp.bfloat16)
            wide.append(dot(value.astype(jnp.bfloat16), source_wide[l]))
        strips = cells // STRIP
        for j in range(strips):
            part = slice(j * STRIP, (j + 1) * STRIP)
            if first:
                copy(j).wait()
            predicted = None
            for l in range(layers):
                for k in range(span):
                    if first:
                        block = tiles[l, k, part, :].T
                        flipped[l, k, :, part] = block
                    else:
                        block = flipped[l, k, :, part]
                    term = dot(wire[l, k], block)
                    predicted = term if predicted is None else predicted + term
            misfit[:, part] = measured[:, part] - predicted
            if j == 0:
                field = far(wide, core_ahead, 1)
        residual = misfit[...] - dot(field, receiver_rows[...])
        misfit[...] = residual
        for offset in range(span):
            sent[slots[offset]] = rolled(residual, RADIUS - offset, own).astype(jnp.bfloat16)
        rounded = residual.astype(jnp.bfloat16)
        wide = [dot(rounded, receiver_wide[l]) for l in range(layers)]
        for l in range(layers):
            for j in range(cells // CHUNK):
                part = slice(j * CHUNK, (j + 1) * CHUNK)
                gradient = None
                for k in range(span):
                    term = dot(sent[k], tiles[l, k, :, part])
                    gradient = term if gradient is None else gradient + term
                if l + j == 0:
                    back = far(wide, core_back, -1)
                gradient = gradient + dot(back, source_rows[l, :, part])
                value = model[l, :, part]
                model[l, :, part] = value + STEP * (gradient - DAMPING * value)

    step(True)
    lax.fori_loop(1, ITERS, lambda index, carry: (step(False), carry)[1], 0)
    if paired:
        packed_out[:, :cells] = merged(model[0], model[1], own).astype(packed_out.dtype)
        packed_out[:, cells:] = merged(misfit[:, :share], misfit[:, share:], own).astype(
            packed_out.dtype
        )
    else:
        for l in range(layers):
            rows = slice(l * cols, (l + 1) * cols)
            packed_out[rows, :cells] = model[l].astype(packed_out.dtype)
            packed_out[rows, cells:] = misfit[:, l * share : (l + 1) * share].astype(
                packed_out.dtype
            )


def whole_array():
    return pl.BlockSpec(memory_space=pltpu.VMEM)


def on_device(
    near_tiles, near_order, receiver_basis, source_basis, coupling, initial_model, observed, *, bands
):
    layers, perts, cells = initial_model.shape
    rank = coupling.shape[-1]
    own = -(-perts // bands)
    held = layers * own
    rows = bands * held
    width = cells + cells // layers
    cols = bands * own
    bf16, f32 = jnp.bfloat16, jnp.float32

    paired = layers == 2 and layers * own == 8 and perts == cols
    small = pltpu.CompilerParams(vmem_limit_bytes=SMALL)
    if paired:
        packed = pl.pallas_call(
            functools.partial(pack_kernel, own=own),
            out_shape=jax.ShapeDtypeStruct((rows, width), bf16),
            in_specs=[whole_array()] * 2,
            out_specs=whole_array(),
            compiler_params=small,
            name="pack",
        )(initial_model, observed)
    else:
        padding = cols - perts
        parts = jnp.pad(initial_model, ((0, 0), (0, padding), (0, 0)))
        parts = parts.reshape(layers, bands, own, cells).transpose(1, 0, 2, 3)
        data = jnp.pad(observed, ((0, padding), (0, 0)))
        data = data.reshape(bands, own, layers, cells // layers).transpose(0, 2, 1, 3)
        packed = jnp.concatenate([parts, data], -1)
    received = lax.all_to_all(packed.reshape(bands, held, width), "row", 0, 0, tiled=True)
    if not paired:
        received = received.reshape(bands, layers, own, width).transpose(1, 0, 2, 3)

    span = near_tiles.shape[1]
    tables = pl.pallas_call(
        tables_kernel,
        out_shape=[
            jax.ShapeDtypeStruct((layers, cells, LANES), bf16),
            jax.ShapeDtypeStruct((layers, cells, LANES), bf16),
            jax.ShapeDtypeStruct((layers, bands * rank, LANES), f32),
            jax.ShapeDtypeStruct((layers, bands * rank, LANES), f32),
            jax.ShapeDtypeStruct((LANES, cells), bf16),
            jax.ShapeDtypeStruct((layers, LANES, cells), bf16),
        ],
        in_specs=[whole_array()] * 4,
        out_specs=[whole_array()] * 6,
        compiler_params=small,
        name="tables",
    )(
        source_basis.transpose(0, 2, 1),
        receiver_basis.transpose(0, 2, 1),
        coupling.transpose(0, 1, 3, 2).reshape(layers, bands * rank, rank),
        coupling.reshape(layers, bands * rank, rank),
    )

    limit = 4 * near_tiles.size + 40 * 4 * cols * cells
    result = pl.pallas_call(
        functools.partial(steps_kernel, bands=bands, own=own, rank=rank, paired=paired),
        out_shape=jax.ShapeDtypeStruct((rows, width), bf16),
        in_specs=[
            pl.BlockSpec(memory_space=pltpu.SMEM),
            whole_array(),
            pl.BlockSpec(memory_space=pl.ANY),
        ]
        + [whole_array()] * 6,
        out_specs=whole_array(),
        scratch_shapes=[
            pltpu.VMEM((layers, cols, cells), f32),
            pltpu.VMEM((cols, cells), f32),
            pltpu.VMEM((cols, cells), f32),
            pltpu.VMEM((layers, span, cols, cells), bf16),
            pltpu.VMEM(near_tiles.shape, bf16),
            pltpu.VMEM(near_tiles.shape, bf16),
            pltpu.SemaphoreType.DMA((cells // STRIP,)),
        ],
        compiler_params=pltpu.CompilerParams(vmem_limit_bytes=limit),
        name="steps",
    )(
        near_order,
        received.reshape(rows, width),
        near_tiles,
        *tables,
    )
    if not paired:
        result = result.reshape(layers, bands, own, width).transpose(1, 0, 2, 3)
    returned = lax.all_to_all(result.reshape(bands, held, width), "row", 0, 0, tiled=True)
    if paired:
        return pl.pallas_call(
            functools.partial(unpack_kernel, own=own),
            out_shape=(
                jax.ShapeDtypeStruct((layers, perts, cells), f32),
                jax.ShapeDtypeStruct((perts, cells), f32),
            ),
            in_specs=[whole_array()],
            out_specs=(whole_array(), whole_array()),
            compiler_params=small,
            name="unpack",
        )(returned.reshape(rows, width))
    returned = returned.reshape(bands, layers, own, width).astype(f32)
    model = returned[..., :cells].transpose(1, 0, 2, 3).reshape(layers, cols, cells)
    misfit = returned[..., cells:].transpose(0, 2, 1, 3).reshape(cols, cells)
    return model[:, :perts], misfit[:perts]


def solution(mesh):
    placed = (P(), P(), P(), P(), P(), P(None, "group", "row"), P("group", "row"))
    return jax.shard_map(
        functools.partial(on_device, bands=mesh.shape["row"]),
        mesh=mesh,
        in_specs=placed,
        out_specs=(P(None, "group", "row"), P("group", "row")),
        check_vma=False,
    )
```

time: 76.2 us -> 68 us (0.89)
  Pallas kernels: 41.2 us -> 30.1 us
  local copies, waits for them, and re-layouts: 2.53 us -> 6.2 us
  blocking collectives: 16.4 us -> 15.4 us
    pallas_call x1, Pallas kernels: 34.3 us -> 27.6 us  [on_device(): pl.pallas_call(functools.partial(steps_kernel, bands=bands, own=own, rank...]
    unnamed x2 -> x12, local copies, waits for them, and re-layouts: 0.74 us -> 5.13 us
    pallas_call x2, Pallas kernels: 4.04 us -> 1.78 us  [the longest x1 0.95 us: on_device(): pl.pallas_call(functools.partial(unpack_kernel, own=own), out_shape=(jax....]
    pallas_call x1, Pallas kernels: 2.82 us -> 0.67 us  [on_device(): pl.pallas_call(tables_kernel, out_shape=[jax.ShapeDtypeStruct((layers, ce...]
    all_to_all x1, blocking collectives: 16.4 us -> 15.4 us  [on_device(): lax.all_to_all(result.reshape(bands, held, width), 'row', 0, 0, tiled=True)]
  transfers between devices with their start and end apart: 1 -> 1, of which waited for: 1 -> 1; matrix products, arithmetic and copies ran while one was open for 2% -> 2% of each run, Pallas kernels for 4% -> 1%
where the time goes in v2:
time: 68 us; the launch traced here: 67.5 us
  Pallas kernels  30.1 us (44%)
  blocking collectives  15.4 us (23%)
  waiting for transfers between devices  7.76 us (11%)
  starting transfers between devices  7.41 us (11%)
  local copies, waits for them, and re-layouts  6.2 us (9%)
  between operations  0.68 us (1%)
    pallas_call x1, Pallas kernels, on_device(): pl.pallas_call(functools.partial(steps_kernel, bands=bands, own=own, rank...  27.6 us
    all_to_all x1, blocking collectives, on_device(): lax.all_to_all(result.reshape(bands, held, width), 'row', 0, 0, tiled=True)  15.4 us
    all_to_all x1, waiting for transfers between devices, on_device(): lax.all_to_all(packed.reshape(bands, held, width), 'row', 0, 0, tiled=True)  7.76 us
    all_to_all x1, starting transfers between devices, on_device(): lax.all_to_all(packed.reshape(bands, held, width), 'row', 0, 0, tiled=True)  7.41 us
    unnamed x12, local copies, waits for them, and re-layouts  5.13 us
  transfers between devices with their start and end apart: 1, of which 1 were waited for; matrix products, arithmetic and copies ran while one was open for 2% of the time, Pallas kernels for 1%

profile of v2, /device:TPU:0, one launch (start us, length us, event | category | flops | bytes accessed | tf_op | source)
XLA Modules:
  0.0 67.5 jit_solution(7027523120291862937)
XLA Ops:
  0.6 0.0 copy-start.1
  0.6 0.9 %copy-done.1 = bf16[2,64,1024]{2,1,0:T(8,128)(2,1)S(1)} copy-done((bf16[2,64,1024]{2,1,0:T(8,128)(2,1)S(1)}, bf16[2,64,1024]{2,1,0:T(8,128)(2,1)}, u32[]{:S(2)}) %copy-start.1) | copy-done | bytes 262168
  1.6 0.0 copy-start.2
  1.6 0.9 %copy-done.2 = bf16[64,1024]{1,0:T(8,128)(2,1)S(1)} copy-done((bf16[64,1024]{1,0:T(8,128)(2,1)S(1)}, bf16[64,1024]{1,0:T(8,128)(2,1)}, u32[]{:S(2)}) %copy-start.2) | copy-done | bytes 131096
  2.5 0.8 %pack.1 = bf16[128,1536]{1,0:T(8,128)(2,1)} custom-call(bf16[2,64,1024]{2,1,0:T(8,128)(2,1)S(1)} %copy-done.1, bf16[64,1024]{1,0:T(8,128)(2,1)S(1)} %copy-done.2), custom_call_target="tpu_custom_call" | custom-call | tf_op jit(solution)/shard_map/pack/pallas_call | solution.py:288
  3.3 7.4 %all-to-all-start = ((bf16[16,8,1536]{2,1,0:T(8,128)(2,1)}), bf16[16,8,1536]{2,1,0:T(8,128)(2,1)S(1)}, u32[]{:S(2)}, u32[]{:S(2)}) async-start(bf16[16,8,1536]{2,1,0:T(8,128)(2,1)} %bitcast), calls=%async_computation | async-start | bytes 786432 | tf_op jit(solution)/shard_map/all_to_all | solution.py:303
  10.7 1.1 %copy.9 = f32[2,16,16,16]{3,2,1,0:T(8,128)S(1)} copy(f32[2,16,16,16]{2,3,1,0:T(8,128)} %bitcast.12) | data formatting | bytes 65536 | tf_op jit(solution)/shard_map/transpose | solution.py:325
  11.8 0.0 copy-start
  11.8 0.9 %copy-done = f32[2,16,16,16]{3,2,1,0:T(8,128)S(1)} copy-done((f32[2,16,16,16]{3,2,1,0:T(8,128)S(1)}, f32[2,16,16,16]{3,2,1,0:T(8,128)}, u32[]{:S(2)}) %copy-start) | copy-done | bytes 32792
  12.8 0.0 copy-start.3
  12.8 0.8 %copy-done.3 = bf16[2,1024,16]{1,2,0:T(8,128)(2,1)S(1)} copy-done((bf16[2,1024,16]{1,2,0:T(8,128)(2,1)S(1)}, bf16[2,1024,16]{1,2,0:T(8,128)(2,1)}, u32[]{:S(2)}) %copy-start.3) | copy-done | bytes 65560
  13.6 0.0 copy-start.4
  13.6 0.8 %copy-done.4 = bf16[2,1024,16]{1,2,0:T(8,128)(2,1)S(1)} copy-done((bf16[2,1024,16]{1,2,0:T(8,128)(2,1)S(1)}, bf16[2,1024,16]{1,2,0:T(8,128)(2,1)}, u32[]{:S(2)}) %copy-start.4) | copy-done | bytes 65560
  14.5 0.7 tables.1
  15.1 7.8 %all-to-all-done = bf16[16,8,1536]{2,1,0:T(8,128)(2,1)S(1)} async-done(((bf16[16,8,1536]{2,1,0:T(8,128)(2,1)}), bf16[16,8,1536]{2,1,0:T(8,128)(2,1)S(1)}, u32[]{:S(2)}, u32[]{:S(2)}) %all-to-all-start) | async-done | bytes 393248 | tf_op jit(solution)/shard_map/all_to_all | solution.py:303
  22.9 0.0 copy-start.5
  22.9 0.7 copy-done.5
  23.6 27.6 %steps.1 = bf16[128,1536]{1,0:T(8,128)(2,1)S(1)} custom-call(s32[5]{0:T(128)S(1)} %copy-done.5, bf16[128,1536]{1,0:T(8,128)(2,1)S(1)} %bitcast.10, bf16[2,5,1024,1024]{3,2,1,0:T(8,128)(2,1)} %tiles_hbm.1, bf16[2,1024,128]{2,1,0:T(8,128)(2,1)S(1)} %get-tuple-element.8.source_wide, bf16[2,1024,128]{2,1,0:T(8,128)(2,1)S(1)} %get-tuple-element.9.receiver_wide, ...), custom_call_target="tpu_custom_call" | custom-call | tf_op jit(solution)/shard_map/steps/pallas_call | solution.py:330
  51.2 15.4 %all_to_all.10 = bf16[16,8,1536]{2,1,0:T(8,128)(2,1)S(1)} all-to-all(bf16[16,8,1536]{2,1,0:T(8,128)(2,1)S(1)} %bitcast.11), channel_id=1, replica_groups=mesh['group'=2,'row'=16] {'row'}, dimensions={0} | all-to-all | bytes 786432 | tf_op jit(solution)/shard_map/all_to_all | solution.py:359
  66.6 0.9 %unpack.1 = (f32[2,64,1024]{2,1,0:T(8,128)}, f32[64,1024]{1,0:T(8,128)}) custom-call(bf16[128,1536]{1,0:T(8,128)(2,1)S(1)} %bitcast.9), custom_call_target="tpu_custom_call" | custom-call | tf_op jit(solution)/shard_map/unpack/pallas_call | solution.py:361
Async XLA Ops:
  0.6 1.0 %copy-start.1 = (bf16[2,64,1024]{2,1,0:T(8,128)(2,1)S(1)}, bf16[2,64,1024]{2,1,0:T(8,128)(2,1)}, u32[]{:S(2)}) copy-start(bf16[2,64,1024]{2,1,0:T(8,128)(2,1)} %model_ref.1) | copy-start | bytes 786436
  1.6 0.9 %copy-start.2 = (bf16[64,1024]{1,0:T(8,128)(2,1)S(1)}, bf16[64,1024]{1,0:T(8,128)(2,1)}, u32[]{:S(2)}) copy-start(bf16[64,1024]{1,0:T(8,128)(2,1)} %data_ref.1) | copy-start | bytes 393220
  3.3 19.6 %all-to-all-start = ((bf16[16,8,1536]{2,1,0:T(8,128)(2,1)}), bf16[16,8,1536]{2,1,0:T(8,128)(2,1)S(1)}, u32[]{:S(2)}, u32[]{:S(2)}) async-start(bf16[16,8,1536]{2,1,0:T(8,128)(2,1)} %bitcast), calls=%async_computation | async-start | bytes 786432 | tf_op jit(solution)/shard_map/all_to_all | solution.py:303
  11.8 1.0 %copy-start = (f32[2,16,16,16]{3,2,1,0:T(8,128)S(1)}, f32[2,16,16,16]{3,2,1,0:T(8,128)}, u32[]{:S(2)}) copy-start(f32[2,16,16,16]{3,2,1,0:T(8,128)} %param.11) | copy-start | bytes 98308
  12.8 0.8 %copy-start.3 = (bf16[2,1024,16]{1,2,0:T(8,128)(2,1)S(1)}, bf16[2,1024,16]{1,2,0:T(8,128)(2,1)}, u32[]{:S(2)}) copy-start(bf16[2,1024,16]{1,2,0:T(8,128)(2,1)} %param.10) | copy-start | bytes 196612
  13.6 0.8 %copy-start.4 = (bf16[2,1024,16]{1,2,0:T(8,128)(2,1)S(1)}, bf16[2,1024,16]{1,2,0:T(8,128)(2,1)}, u32[]{:S(2)}) copy-start(bf16[2,1024,16]{1,2,0:T(8,128)(2,1)} %param.9) | copy-start | bytes 196612
  22.9 0.7 copy-start.5

commit v3 on v2

--- a/solution.py
+++ b/solution.py
@@ -15,6 +15,7 @@
 COPIES = 3
 LANES = 128
 STRIP = 256
+EARLY = 2
 CHUNK = 512
 SMALL = 8 << 20
 
@@ -35,11 +36,10 @@
     )
 
 
-def tables_kernel(
+def tables(
     source_ref,
     receiver_ref,
-    ahead_ref,
-    back_ref,
+    coupling_ref,
     source_wide,
     receiver_wide,
     core_ahead,
@@ -58,28 +58,28 @@
         source_wide[l] = jnp.concatenate([source_ref[l]] * (LANES // rank), 0).T
         receiver_wide[l] = jnp.concatenate([receiver_ref[l]] * (LANES // rank), 0).T
         before, after = l * COPIES * rank, LANES - (l + 1) * COPIES * rank
-        for narrow, out in ((ahead_ref, core_ahead), (back_ref, core_back)):
-            block = narrow[l]
+        back = coupling_ref[l]
+        count = back.shape[0]
+        turned = jnp.concatenate([back, jnp.zeros((count, LANES - rank), jnp.float32)], 1).T
+        ahead = jnp.concatenate(
+            [turned[:rank, first : first + rank] for first in range(0, count, rank)], 0
+        )
+        for block, out in ((ahead, core_ahead), (back, core_back)):
             parts = [block] * COPIES
             if before:
-                parts = [jnp.zeros((block.shape[0], before), jnp.float32)] + parts
-            parts = parts + [jnp.zeros((block.shape[0], after), jnp.float32)]
+                parts = [jnp.zeros((count, before), jnp.float32)] + parts
+            parts = parts + [jnp.zeros((count, after), jnp.float32)]
             out[l] = jnp.concatenate(parts, 1)
 
 
-def exchanged(first, second, own):
-    shape = first.shape
-    first = first.reshape(-1, 2 * own, shape[-1])
-    second = second.reshape(-1, 2 * own, shape[-1])
+def merged(first, second, own):
+    lanes = first.shape[-1]
+    first = first.reshape(-1, 2 * own, lanes)
+    second = second.reshape(-1, 2 * own, lanes)
     low = lax.broadcasted_iota(jnp.int32, first.shape, 1) < own
     even = jnp.where(low, first, pltpu.roll(second, own, 1))
     odd = jnp.where(low, pltpu.roll(first, own, 1), second)
-    return even, odd
-
-
-def merged(first, second, own):
-    even, odd = exchanged(first, second, own)
-    return jnp.stack([even, odd], 1).reshape(-1, first.shape[-1])
+    return jnp.stack([even, odd], 1).reshape(-1, lanes)
 
 
 def parted(values, own):
@@ -91,16 +91,88 @@
     return first.reshape(-1, values.shape[-1]), second.reshape(-1, values.shape[-1])
 
 
-def pack_kernel(model_ref, data_ref, out_ref, *, own):
+def pack_kernel(model_hbm, data_hbm, out_ref, model_ref, data_ref, sems, *, own):
     cells = model_ref.shape[-1]
     half = cells // 2
     f32 = jnp.float32
+    model_copy = pltpu.make_async_copy(model_hbm, model_ref, sems.at[0])
+    data_copy = pltpu.make_async_copy(data_hbm, data_ref, sems.at[1])
+    model_copy.start()
+    data_copy.start()
+    model_copy.wait()
     out_ref[:, :cells] = merged(
         model_ref[0].astype(f32), model_ref[1].astype(f32), own
     ).astype(out_ref.dtype)
+    data_copy.wait()
     out_ref[:, cells:] = merged(
         data_ref[:, :half].astype(f32), data_ref[:, half:].astype(f32), own
     ).astype(out_ref.dtype)
+
+
+def ready_kernel(
+    source_hbm,
+    receiver_hbm,
+    coupling_hbm,
+    tiles_hbm,
+    source_wide,
+    receiver_wide,
+    core_ahead,
+    core_back,
+    receiver_rows,
+    source_rows,
+    flipped_hbm,
+    source_ref,
+    receiver_ref,
+    coupling_ref,
+    natural,
+    flipped,
+    small_sems,
+    in_sems,
+    out_sems,
+):
+    layers = tiles_hbm.shape[0]
+    small = [
+        pltpu.make_async_copy(source, target, small_sems.at[n])
+        for n, (source, target) in enumerate(
+            (
+                (source_hbm, source_ref),
+                (receiver_hbm, receiver_ref),
+                (coupling_hbm, coupling_ref),
+            )
+        )
+    ]
+    pairs = [(l, k) for l in range(layers) for k in range(EARLY)]
+    arrive = [
+        pltpu.make_async_copy(tiles_hbm.at[l, k], natural.at[l, k], in_sems.at[n])
+        for n, (l, k) in enumerate(pairs)
+    ]
+    leave = [
+        pltpu.make_async_copy(flipped.at[l, k], flipped_hbm.at[l, k], out_sems.at[n])
+        for n, (l, k) in enumerate(pairs)
+    ]
+    for copy in small + arrive:
+        copy.start()
+    for n, (l, k) in enumerate(pairs):
+        arrive[n].wait()
+        for first in range(0, natural.shape[2], STRIP):
+            part = slice(first, first + STRIP)
+            flipped[l, k, :, part] = natural[l, k, part, :].T
+        leave[n].start()
+    for copy in small:
+        copy.wait()
+    tables(
+        source_ref,
+        receiver_ref,
+        coupling_ref,
+        source_wide,
+        receiver_wide,
+        core_ahead,
+        core_back,
+        receiver_rows,
+        source_rows,
+    )
+    for copy in leave:
+        copy.wait()
 
 
 def unpack_kernel(in_ref, model_ref, data_ref, *, own):
@@ -136,9 +208,10 @@
 
 
 def steps_kernel(
-    order_ref,
+    order_hbm,
     packed_in,
     tiles_hbm,
+    flipped_hbm,
     source_wide,
     receiver_wide,
     core_ahead,
@@ -150,9 +223,13 @@
     measured,
     misfit,
     wire,
+    sent,
     tiles,
     flipped,
-    sems,
+    order_ref,
+    order_sem,
+    strip_sems,
+    late_sems,
     *,
     bands,
     own,
@@ -164,14 +241,29 @@
     share = cells // layers
     cols = bands * own
 
-    def copy(j):
+    strips = cells // STRIP
+
+    def piece(j, l, k):
         part = pl.ds(j * STRIP, STRIP)
-        return pltpu.make_async_copy(
-            tiles_hbm.at[:, :, part, :], tiles.at[:, :, part, :], sems.at[j]
-        )
-
-    for j in range(cells // STRIP):
-        copy(j).start()
+        sem = strip_sems.at[j, l, k]
+        if k < EARLY:
+            return pltpu.make_async_copy(
+                flipped_hbm.at[l, k, :, part], flipped.at[l, k, :, part], sem
+            )
+        return pltpu.make_async_copy(tiles_hbm.at[l, k, part, :], tiles.at[l, k, part, :], sem)
+
+    def late(l, k):
+        return pltpu.make_async_copy(tiles_hbm.at[l, k], tiles.at[l, k], late_sems.at[l, k])
+
+    order = pltpu.make_async_copy(order_hbm, order_ref, order_sem)
+    order.start()
+    for j in range(strips):
+        for l in range(layers):
+            for k in range(span):
+                piece(j, l, k).start()
+    for l in range(layers):
+        for k in range(EARLY):
+            late(l, k).start()
     if paired:
         model[0], model[1] = parted(packed_in[:, :cells].astype(jnp.float32), own)
         measured[:, :share], measured[:, share:] = parted(
@@ -183,7 +275,7 @@
             model[l] = packed_in[rows, :cells].astype(jnp.float32)
             measured[:, l * share : (l + 1) * share] = packed_in[rows, cells:].astype(jnp.float32)
 
-    sent = wire.at[0]
+    order.wait()
     slots = []
     for offset in range(span):
         slot = jnp.int32(0)
@@ -206,22 +298,21 @@
             total = lax.fori_loop(0, groups, add, (stair, total), unroll=groups <= 2)[1]
         return split_parts(total, rank)
 
+    def send(l):
+        value = model[l]
+        for offset in range(span):
+            wire[l, slots[offset]] = rolled(value, offset - RADIUS, own).astype(jnp.bfloat16)
+
     def step(first):
-        wide = []
-        for l in range(layers):
-            value = model[l]
-            for offset in range(span):
-                wire[l, slots[offset]] = rolled(value, offset - RADIUS, own).astype(jnp.bfloat16)
-            wide.append(dot(value.astype(jnp.bfloat16), source_wide[l]))
-        strips = cells // STRIP
+        wide = [dot(model[l].astype(jnp.bfloat16), source_wide[l]) for l in range(layers)]
         for j in range(strips):
             part = slice(j * STRIP, (j + 1) * STRIP)
-            if first:
-                copy(j).wait()
             predicted = None
             for l in range(layers):
                 for k in range(span):
                     if first:
+                        piece(j, l, k).wait()
+                    if first and k >= EARLY:
                         block = tiles[l, k, part, :].T
                         flipped[l, k, :, part] = block
                     else:
@@ -238,6 +329,9 @@
         rounded = residual.astype(jnp.bfloat16)
         wide = [dot(rounded, receiver_wide[l]) for l in range(layers)]
         for l in range(layers):
+            if first:
+                for k in range(EARLY):
+                    late(l, k).wait()
             for j in range(cells // CHUNK):
                 part = slice(j * CHUNK, (j + 1) * CHUNK)
                 gradient = None
@@ -249,7 +343,10 @@
                 gradient = gradient + dot(back, source_rows[l, :, part])
                 value = model[l, :, part]
                 model[l, :, part] = value + STEP * (gradient - DAMPING * value)
-
+            send(l)
+
+    for l in range(layers):
+        send(l)
     step(True)
     lax.fori_loop(1, ITERS, lambda index, carry: (step(False), carry)[1], 0)
     if paired:
@@ -270,6 +367,14 @@
     return pl.BlockSpec(memory_space=pltpu.VMEM)
 
 
+def in_place():
+    return pl.BlockSpec(memory_space=pltpu.HBM)
+
+
+def stay(value):
+    return pltpu.with_memory_space_constraint(value, pltpu.HBM)
+
+
 def on_device(
     near_tiles, near_order, receiver_basis, source_basis, coupling, initial_model, observed, *, bands
 ):
@@ -284,15 +389,21 @@
 
     paired = layers == 2 and layers * own == 8 and perts == cols
     small = pltpu.CompilerParams(vmem_limit_bytes=SMALL)
+    span = near_tiles.shape[1]
     if paired:
         packed = pl.pallas_call(
             functools.partial(pack_kernel, own=own),
             out_shape=jax.ShapeDtypeStruct((rows, width), bf16),
-            in_specs=[whole_array()] * 2,
+            in_specs=[in_place()] * 2,
             out_specs=whole_array(),
+            scratch_shapes=[
+                pltpu.VMEM(initial_model.shape, bf16),
+                pltpu.VMEM(observed.shape, bf16),
+                pltpu.SemaphoreType.DMA((2,)),
+            ],
             compiler_params=small,
             name="pack",
-        )(initial_model, observed)
+        )(stay(initial_model), stay(observed))
     else:
         padding = cols - perts
         parts = jnp.pad(initial_model, ((0, 0), (0, padding), (0, 0)))
@@ -304,9 +415,14 @@
     if not paired:
         received = received.reshape(bands, layers, own, width).transpose(1, 0, 2, 3)
 
-    span = near_tiles.shape[1]
-    tables = pl.pallas_call(
-        tables_kernel,
+    factors = [
+        source_basis.transpose(0, 2, 1),
+        receiver_basis.transpose(0, 2, 1),
+        coupling.reshape(layers, bands * rank, rank),
+    ]
+    early = (layers, EARLY, cells, cells)
+    *prepared, flipped_early = pl.pallas_call(
+        ready_kernel,
         out_shape=[
             jax.ShapeDtypeStruct((layers, cells, LANES), bf16),
             jax.ShapeDtypeStruct((layers, cells, LANES), bf16),
@@ -314,26 +430,30 @@
             jax.ShapeDtypeStruct((layers, bands * rank, LANES), f32),
             jax.ShapeDtypeStruct((LANES, cells), bf16),
             jax.ShapeDtypeStruct((layers, LANES, cells), bf16),
+            pltpu.HBM(early, bf16),
         ],
-        in_specs=[whole_array()] * 4,
-        out_specs=[whole_array()] * 6,
-        compiler_params=small,
-        name="tables",
-    )(
-        source_basis.transpose(0, 2, 1),
-        receiver_basis.transpose(0, 2, 1),
-        coupling.transpose(0, 1, 3, 2).reshape(layers, bands * rank, rank),
-        coupling.reshape(layers, bands * rank, rank),
-    )
-
+        in_specs=[in_place()] * 4,
+        out_specs=[whole_array()] * 6 + [in_place()],
+        scratch_shapes=[pltpu.VMEM(value.shape, value.dtype) for value in factors]
+        + [
+            pltpu.VMEM(early, bf16),
+            pltpu.VMEM(early, bf16),
+            pltpu.SemaphoreType.DMA((3,)),
+            pltpu.SemaphoreType.DMA((layers * EARLY,)),
+            pltpu.SemaphoreType.DMA((layers * EARLY,)),
+        ],
+        compiler_params=pltpu.CompilerParams(vmem_limit_bytes=24 << 20),
+        name="ready",
+    )(*[stay(value) for value in factors], stay(near_tiles))
     limit = 4 * near_tiles.size + 40 * 4 * cols * cells
     result = pl.pallas_call(
         functools.partial(steps_kernel, bands=bands, own=own, rank=rank, paired=paired),
         out_shape=jax.ShapeDtypeStruct((rows, width), bf16),
         in_specs=[
-            pl.BlockSpec(memory_space=pltpu.SMEM),
+            in_place(),
             whole_array(),
-            pl.BlockSpec(memory_space=pl.ANY),
+            in_place(),
+            in_place(),
         ]
         + [whole_array()] * 6,
         out_specs=whole_array(),
@@ -342,17 +462,22 @@
             pltpu.VMEM((cols, cells), f32),
             pltpu.VMEM((cols, cells), f32),
             pltpu.VMEM((layers, span, cols, cells), bf16),
+            pltpu.VMEM((span, cols, cells), bf16),
             pltpu.VMEM(near_tiles.shape, bf16),
             pltpu.VMEM(near_tiles.shape, bf16),
-            pltpu.SemaphoreType.DMA((cells // STRIP,)),
+            pltpu.SMEM((span,), jnp.int32),
+            pltpu.SemaphoreType.DMA,
+            pltpu.SemaphoreType.DMA((cells // STRIP, layers, span)),
+            pltpu.SemaphoreType.DMA((layers, EARLY)),
         ],
         compiler_params=pltpu.CompilerParams(vmem_limit_bytes=limit),
         name="steps",
     )(
-        near_order,
+        stay(near_order),
         received.reshape(rows, width),
-        near_tiles,
-        *tables,
+        stay(near_tiles),
+        stay(flipped_early),
+        *prepared,
     )
     if not paired:
         result = result.reshape(layers, bands, own, width).transpose(1, 0, 2, 3)

time: 68 us -> 68.3 us (level)
  Pallas kernels: 30.1 us -> 38.9 us
  local copies, waits for them, and re-layouts: 6.2 us -> 0 us
  waiting for transfers between devices: 7.76 us -> 5.68 us
    pallas_call x1, Pallas kernels: 0.67 us -> 6.48 us  [on_device(): pl.pallas_call(ready_kernel, out_shape=[jax.ShapeDtypeStruct((layers, cel...]
    unnamed x12 -> x0, local copies, waits for them, and re-layouts: 5.13 us -> none
    all_to_all x1, waiting for transfers between devices: 7.76 us -> 5.68 us  [on_device(): lax.all_to_all(packed.reshape(bands, held, width), 'row', 0, 0, tiled=True)]
    pallas_call x1, Pallas kernels: 27.6 us -> 29.6 us  [on_device(): pl.pallas_call(functools.partial(steps_kernel, bands=bands, own=own, rank...]
    transpose x1 -> x0, local copies, waits for them, and re-layouts: 1.07 us -> none  [on_device(): coupling.transpose(0, 1, 3, 2).reshape(layers, bands * rank, rank)]
    pallas_call x1, Pallas kernels: 0.84 us -> 1.81 us  [on_device(): pl.pallas_call(functools.partial(pack_kernel, own=own), out_shape=jax.Sha...]
  transfers between devices with their start and end apart: 1 -> 1, of which waited for: 1 -> 1; matrix products, arithmetic and copies ran while one was open for 2% -> 0% of each run, Pallas kernels for 1% -> 10%
where the time goes in v3:
time: 68.3 us; the launch traced here: 68 us
  Pallas kernels  38.9 us (57%)
  blocking collectives  15.4 us (23%)
  starting transfers between devices  7.43 us (11%)
  waiting for transfers between devices  5.68 us (8%)
    pallas_call x1, Pallas kernels, on_device(): pl.pallas_call(functools.partial(steps_kernel, bands=bands, own=own, rank...  29.6 us
    all_to_all x1, blocking collectives, on_device(): lax.all_to_all(result.reshape(bands, held, width), 'row', 0, 0, tiled=True)  15.4 us
    all_to_all x1, starting transfers between devices, on_device(): lax.all_to_all(packed.reshape(bands, held, width), 'row', 0, 0, tiled=True)  7.43 us
    pallas_call x1, Pallas kernels, on_device(): pl.pallas_call(ready_kernel, out_shape=[jax.ShapeDtypeStruct((layers, cel...  6.48 us
    all_to_all x1, waiting for transfers between devices, on_device(): lax.all_to_all(packed.reshape(bands, held, width), 'row', 0, 0, tiled=True)  5.68 us
    pallas_call x1, Pallas kernels, on_device(): pl.pallas_call(functools.partial(pack_kernel, own=own), out_shape=jax.Sha...  1.81 us
  transfers between devices with their start and end apart: 1, of which 1 were waited for; matrix products, arithmetic and copies ran while one was open for 0% of the time, Pallas kernels for 10%

profile of v3, /device:TPU:0, one launch (start us, length us, event | category | flops | bytes accessed | tf_op | source)
XLA Modules:
  0.0 68.0 jit_solution(4800885480228277141)
XLA Ops:
  0.6 1.8 %pack.1 = bf16[128,1536]{1,0:T(8,128)(2,1)} custom-call(bf16[2,64,1024]{2,1,0:T(8,128)(2,1)} %model_hbm.1, bf16[64,1024]{1,0:T(8,128)(2,1)} %data_hbm.1), custom_call_target="tpu_custom_call" | custom-call | tf_op jit(solution)/shard_map/pack/pallas_call | solution.py:394
  2.4 7.4 %all-to-all-start = ((bf16[16,8,1536]{2,1,0:T(8,128)(2,1)}), bf16[16,8,1536]{2,1,0:T(8,128)(2,1)S(1)}, u32[]{:S(2)}, u32[]{:S(2)}) async-start(bf16[16,8,1536]{2,1,0:T(8,128)(2,1)} %bitcast), calls=%async_computation | async-start | bytes 786432 | tf_op jit(solution)/shard_map/all_to_all | solution.py:414
  9.9 6.5 %ready.1 = (bf16[2,1024,128]{2,1,0:T(8,128)(2,1)S(1)}, bf16[2,1024,128]{2,1,0:T(8,128)(2,1)S(1)}, f32[2,256,128]{2,1,0:T(8,128)S(1)}, f32[2,256,128]{2,1,0:T(8,1...) custom-call(bf16[2,16,1024]{2,1,0:T(8,128)(2,1)} %bitcast.11, ...), custom_call_target="tpu_custom_call" | custom-call | tf_op jit(solution)/shard_map/ready/pallas_call | solution.py:424
  16.4 5.7 %all-to-all-done = bf16[16,8,1536]{2,1,0:T(8,128)(2,1)S(1)} async-done(((bf16[16,8,1536]{2,1,0:T(8,128)(2,1)}), bf16[16,8,1536]{2,1,0:T(8,128)(2,1)S(1)}, u32[]{:S(2)}, u32[]{:S(2)}) %all-to-all-start) | async-done | bytes 393248 | tf_op jit(solution)/shard_map/all_to_all | solution.py:414
  22.0 29.6 %steps.1 = bf16[128,1536]{1,0:T(8,128)(2,1)S(1)} custom-call(s32[5]{0:T(128)} %order_hbm.1, bf16[128,1536]{1,0:T(8,128)(2,1)S(1)} %bitcast.7, bf16[2,5,1024,1024]{3,2,1,0:T(8,128)(2,1)} %tiles_hbm.3, bf16[2,2,1024,1024]{3,2,1,0:T(8,128)(2,1)} %get-tuple-element.9.flipped_hbm, bf16[2,1024,128]{2,1,0:T(8,128)(2,1)S(1)} %get-tuple-element.10.source_wide, ...), custom_call_target="tpu_custom_call" | custom-call | tf_op jit(solution)/shard_map/steps/pallas_call | solution.py:449
  51.7 15.4 %all_to_all.10 = bf16[16,8,1536]{2,1,0:T(8,128)(2,1)S(1)} all-to-all(bf16[16,8,1536]{2,1,0:T(8,128)(2,1)S(1)} %bitcast.8), channel_id=1, replica_groups=mesh['group'=2,'row'=16] {'row'}, dimensions={0} | all-to-all | bytes 786432 | tf_op jit(solution)/shard_map/all_to_all | solution.py:484
  67.1 0.9 %unpack.1 = (f32[2,64,1024]{2,1,0:T(8,128)}, f32[64,1024]{1,0:T(8,128)}) custom-call(bf16[128,1536]{1,0:T(8,128)(2,1)S(1)} %bitcast.9), custom_call_target="tpu_custom_call" | custom-call | tf_op jit(solution)/shard_map/unpack/pallas_call | solution.py:486
Async XLA Ops:
  2.4 19.6 %all-to-all-start = ((bf16[16,8,1536]{2,1,0:T(8,128)(2,1)}), bf16[16,8,1536]{2,1,0:T(8,128)(2,1)S(1)}, u32[]{:S(2)}, u32[]{:S(2)}) async-start(bf16[16,8,1536]{2,1,0:T(8,128)(2,1)} %bitcast), calls=%async_computation | async-start | bytes 786432 | tf_op jit(solution)/shard_map/all_to_all | solution.py:414

commit v4 on v2

--- a/solution.py
+++ b/solution.py
@@ -67,19 +67,14 @@
             out[l] = jnp.concatenate(parts, 1)
 
 
-def exchanged(first, second, own):
-    shape = first.shape
-    first = first.reshape(-1, 2 * own, shape[-1])
-    second = second.reshape(-1, 2 * own, shape[-1])
+def merged(first, second, own):
+    lanes = first.shape[-1]
+    first = first.reshape(-1, 2 * own, lanes)
+    second = second.reshape(-1, 2 * own, lanes)
     low = lax.broadcasted_iota(jnp.int32, first.shape, 1) < own
     even = jnp.where(low, first, pltpu.roll(second, own, 1))
     odd = jnp.where(low, pltpu.roll(first, own, 1), second)
-    return even, odd
-
-
-def merged(first, second, own):
-    even, odd = exchanged(first, second, own)
-    return jnp.stack([even, odd], 1).reshape(-1, first.shape[-1])
+    return jnp.stack([even, odd], 1).reshape(-1, lanes)
 
 
 def parted(values, own):
@@ -91,13 +86,19 @@
     return first.reshape(-1, values.shape[-1]), second.reshape(-1, values.shape[-1])
 
 
-def pack_kernel(model_ref, data_ref, out_ref, *, own):
+def pack_kernel(model_hbm, data_hbm, out_ref, model_ref, data_ref, sems, *, own):
     cells = model_ref.shape[-1]
     half = cells // 2
     f32 = jnp.float32
+    model_copy = pltpu.make_async_copy(model_hbm, model_ref, sems.at[0])
+    data_copy = pltpu.make_async_copy(data_hbm, data_ref, sems.at[1])
+    model_copy.start()
+    data_copy.start()
+    model_copy.wait()
     out_ref[:, :cells] = merged(
         model_ref[0].astype(f32), model_ref[1].astype(f32), own
     ).astype(out_ref.dtype)
+    data_copy.wait()
     out_ref[:, cells:] = merged(
         data_ref[:, :half].astype(f32), data_ref[:, half:].astype(f32), own
     ).astype(out_ref.dtype)
@@ -136,7 +137,7 @@
 
 
 def steps_kernel(
-    order_ref,
+    order_hbm,
     packed_in,
     tiles_hbm,
     source_wide,
@@ -152,6 +153,8 @@
     wire,
     tiles,
     flipped,
+    order_ref,
+    order_sem,
     sems,
     *,
     bands,
@@ -172,6 +175,8 @@
 
     for j in range(cells // STRIP):
         copy(j).start()
+    order = pltpu.make_async_copy(order_hbm, order_ref, order_sem)
+    order.start()
     if paired:
         model[0], model[1] = parted(packed_in[:, :cells].astype(jnp.float32), own)
         measured[:, :share], measured[:, share:] = parted(
@@ -183,6 +188,7 @@
             model[l] = packed_in[rows, :cells].astype(jnp.float32)
             measured[:, l * share : (l + 1) * share] = packed_in[rows, cells:].astype(jnp.float32)
 
+    order.wait()
     sent = wire.at[0]
     slots = []
     for offset in range(span):
@@ -270,6 +276,14 @@
     return pl.BlockSpec(memory_space=pltpu.VMEM)
 
 
+def in_place():
+    return pl.BlockSpec(memory_space=pltpu.HBM)
+
+
+def stay(value):
+    return pltpu.with_memory_space_constraint(value, pltpu.HBM)
+
+
 def on_device(
     near_tiles, near_order, receiver_basis, source_basis, coupling, initial_model, observed, *, bands
 ):
@@ -288,11 +302,16 @@
         packed = pl.pallas_call(
             functools.partial(pack_kernel, own=own),
             out_shape=jax.ShapeDtypeStruct((rows, width), bf16),
-            in_specs=[whole_array()] * 2,
+            in_specs=[in_place()] * 2,
             out_specs=whole_array(),
+            scratch_shapes=[
+                pltpu.VMEM(initial_model.shape, bf16),
+                pltpu.VMEM(observed.shape, bf16),
+                pltpu.SemaphoreType.DMA((2,)),
+            ],
             compiler_params=small,
             name="pack",
-        )(initial_model, observed)
+        )(stay(initial_model), stay(observed))
     else:
         padding = cols - perts
         parts = jnp.pad(initial_model, ((0, 0), (0, padding), (0, 0)))
@@ -331,9 +350,9 @@
         functools.partial(steps_kernel, bands=bands, own=own, rank=rank, paired=paired),
         out_shape=jax.ShapeDtypeStruct((rows, width), bf16),
         in_specs=[
-            pl.BlockSpec(memory_space=pltpu.SMEM),
+            in_place(),
             whole_array(),
-            pl.BlockSpec(memory_space=pl.ANY),
+            in_place(),
         ]
         + [whole_array()] * 6,
         out_specs=whole_array(),
@@ -344,14 +363,16 @@
             pltpu.VMEM((layers, span, cols, cells), bf16),
             pltpu.VMEM(near_tiles.shape, bf16),
             pltpu.VMEM(near_tiles.shape, bf16),
+            pltpu.SMEM((span,), jnp.int32),
+            pltpu.SemaphoreType.DMA,
             pltpu.SemaphoreType.DMA((cells // STRIP,)),
         ],
         compiler_params=pltpu.CompilerParams(vmem_limit_bytes=limit),
         name="steps",
     )(
-        near_order,
+        stay(near_order),
         received.reshape(rows, width),
-        near_tiles,
+        stay(near_tiles),
         *tables,
     )
     if not paired:

time: 68 us -> 65.9 us (0.969)
  local copies, waits for them, and re-layouts: 6.2 us -> 3.7 us
    unnamed x12 -> x6, local copies, waits for them, and re-layouts: 5.13 us -> 2.63 us
    pallas_call x1, Pallas kernels: 0.84 us -> 1.81 us  [on_device(): pl.pallas_call(functools.partial(pack_kernel, own=own), out_shape=jax.Sha...]
where the time goes in v4:
time: 65.9 us; the launch traced here: 65.5 us
  Pallas kernels  30.5 us (46%)
  blocking collectives  15.4 us (23%)
  waiting for transfers between devices  7.76 us (12%)
  starting transfers between devices  7.43 us (11%)
  local copies, waits for them, and re-layouts  3.7 us (6%)
  between operations  0.68 us (1%)
    pallas_call x1, Pallas kernels, on_device(): pl.pallas_call(functools.partial(steps_kernel, bands=bands, own=own, rank...  27.1 us
    all_to_all x1, blocking collectives, on_device(): lax.all_to_all(result.reshape(bands, held, width), 'row', 0, 0, tiled=True)  15.4 us
    all_to_all x1, waiting for transfers between devices, on_device(): lax.all_to_all(packed.reshape(bands, held, width), 'row', 0, 0, tiled=True)  7.76 us
    all_to_all x1, starting transfers between devices, on_device(): lax.all_to_all(packed.reshape(bands, held, width), 'row', 0, 0, tiled=True)  7.43 us
    unnamed x6, local copies, waits for them, and re-layouts  2.63 us
    pallas_call x1, Pallas kernels, on_device(): pl.pallas_call(functools.partial(pack_kernel, own=own), out_shape=jax.Sha...  1.81 us
  transfers between devices with their start and end apart: 1, of which 1 were waited for; matrix products, arithmetic and copies ran while one was open for 2% of the time, Pallas kernels for 1%

profile of v4, /device:TPU:0, one launch (start us, length us, event | category | flops | bytes accessed | tf_op | source)
XLA Modules:
  0.0 65.5 jit_solution(4151643228501659453)
XLA Ops:
  0.6 1.8 %pack.1 = bf16[128,1536]{1,0:T(8,128)(2,1)} custom-call(bf16[2,64,1024]{2,1,0:T(8,128)(2,1)} %model_hbm.1, bf16[64,1024]{1,0:T(8,128)(2,1)} %data_hbm.1), custom_call_target="tpu_custom_call" | custom-call | tf_op jit(solution)/shard_map/pack/pallas_call | solution.py:302
  2.4 7.4 %all-to-all-start = ((bf16[16,8,1536]{2,1,0:T(8,128)(2,1)}), bf16[16,8,1536]{2,1,0:T(8,128)(2,1)S(1)}, u32[]{:S(2)}, u32[]{:S(2)}) async-start(bf16[16,8,1536]{2,1,0:T(8,128)(2,1)} %bitcast), calls=%async_computation | async-start | bytes 786432 | tf_op jit(solution)/shard_map/all_to_all | solution.py:322
  9.9 1.1 %copy.9 = f32[2,16,16,16]{3,2,1,0:T(8,128)S(1)} copy(f32[2,16,16,16]{2,3,1,0:T(8,128)} %bitcast.12) | data formatting | bytes 65536 | tf_op jit(solution)/shard_map/transpose | solution.py:344
  11.0 0.0 copy-start
  11.0 0.9 %copy-done = f32[2,16,16,16]{3,2,1,0:T(8,128)S(1)} copy-done((f32[2,16,16,16]{3,2,1,0:T(8,128)S(1)}, f32[2,16,16,16]{3,2,1,0:T(8,128)}, u32[]{:S(2)}) %copy-start) | copy-done | bytes 32792
  11.9 0.0 copy-start.1
  11.9 0.8 %copy-done.1 = bf16[2,1024,16]{1,2,0:T(8,128)(2,1)S(1)} copy-done((bf16[2,1024,16]{1,2,0:T(8,128)(2,1)S(1)}, bf16[2,1024,16]{1,2,0:T(8,128)(2,1)}, u32[]{:S(2)}) %copy-start.1) | copy-done | bytes 65560
  12.8 0.0 copy-start.2
  12.8 0.8 %copy-done.2 = bf16[2,1024,16]{1,2,0:T(8,128)(2,1)S(1)} copy-done((bf16[2,1024,16]{1,2,0:T(8,128)(2,1)S(1)}, bf16[2,1024,16]{1,2,0:T(8,128)(2,1)}, u32[]{:S(2)}) %copy-start.2) | copy-done | bytes 65560
  13.6 0.7 %tables.1 = (bf16[2,1024,128]{2,1,0:T(8,128)(2,1)S(1)}, bf16[2,1024,128]{2,1,0:T(8,128)(2,1)S(1)}, f32[2,256,128]{2,1,0:T(8,128)S(1)}, f32[2,256,128]{2,1,0:T(8,...) custom-call(bf16[2,16,1024]{2,1,0:T(8,128)(2,1)S(1)} %bitcast.15, ...), custom_call_target="tpu_custom_call" | custom-call | tf_op jit(solution)/shard_map/tables/pallas_call | solution.py:327
  14.3 7.8 %all-to-all-done = bf16[16,8,1536]{2,1,0:T(8,128)(2,1)S(1)} async-done(((bf16[16,8,1536]{2,1,0:T(8,128)(2,1)}), bf16[16,8,1536]{2,1,0:T(8,128)(2,1)S(1)}, u32[]{:S(2)}, u32[]{:S(2)}) %all-to-all-start) | async-done | bytes 393248 | tf_op jit(solution)/shard_map/all_to_all | solution.py:322
  22.0 27.1 %steps.1 = bf16[128,1536]{1,0:T(8,128)(2,1)S(1)} custom-call(s32[5]{0:T(128)} %order_hbm.1, bf16[128,1536]{1,0:T(8,128)(2,1)S(1)} %bitcast.10, bf16[2,5,1024,1024]{3,2,1,0:T(8,128)(2,1)} %tiles_hbm.1, bf16[2,1024,128]{2,1,0:T(8,128)(2,1)S(1)} %get-tuple-element.8.source_wide, bf16[2,1024,128]{2,1,0:T(8,128)(2,1)S(1)} %get-tuple-element.9.receiver_wide, ...), custom_call_target="tpu_custom_call" | custom-call | tf_op jit(solution)/shard_map/steps/pallas_call | solution.py:349
  49.1 15.4 %all_to_all.10 = bf16[16,8,1536]{2,1,0:T(8,128)(2,1)S(1)} all-to-all(bf16[16,8,1536]{2,1,0:T(8,128)(2,1)S(1)} %bitcast.11), channel_id=1, replica_groups=mesh['group'=2,'row'=16] {'row'}, dimensions={0} | all-to-all | bytes 786432 | tf_op jit(solution)/shard_map/all_to_all | solution.py:380
  64.5 0.9 %unpack.1 = (f32[2,64,1024]{2,1,0:T(8,128)}, f32[64,1024]{1,0:T(8,128)}) custom-call(bf16[128,1536]{1,0:T(8,128)(2,1)S(1)} %bitcast.9), custom_call_target="tpu_custom_call" | custom-call | tf_op jit(solution)/shard_map/unpack/pallas_call | solution.py:382
Async XLA Ops:
  2.4 19.6 %all-to-all-start = ((bf16[16,8,1536]{2,1,0:T(8,128)(2,1)}), bf16[16,8,1536]{2,1,0:T(8,128)(2,1)S(1)}, u32[]{:S(2)}, u32[]{:S(2)}) async-start(bf16[16,8,1536]{2,1,0:T(8,128)(2,1)} %bitcast), calls=%async_computation | async-start | bytes 786432 | tf_op jit(solution)/shard_map/all_to_all | solution.py:322
  11.0 1.0 %copy-start = (f32[2,16,16,16]{3,2,1,0:T(8,128)S(1)}, f32[2,16,16,16]{3,2,1,0:T(8,128)}, u32[]{:S(2)}) copy-start(f32[2,16,16,16]{3,2,1,0:T(8,128)} %param.11) | copy-start | bytes 98308
  11.9 0.8 %copy-start.1 = (bf16[2,1024,16]{1,2,0:T(8,128)(2,1)S(1)}, bf16[2,1024,16]{1,2,0:T(8,128)(2,1)}, u32[]{:S(2)}) copy-start(bf16[2,1024,16]{1,2,0:T(8,128)(2,1)} %param.10) | copy-start | bytes 196612
  12.8 0.8 %copy-start.2 = (bf16[2,1024,16]{1,2,0:T(8,128)(2,1)S(1)}, bf16[2,1024,16]{1,2,0:T(8,128)(2,1)}, u32[]{:S(2)}) copy-start(bf16[2,1024,16]{1,2,0:T(8,128)(2,1)} %param.9) | copy-start | bytes 196612

commit v5 on v4

--- a/solution.py
+++ b/solution.py
@@ -167,14 +167,15 @@
     share = cells // layers
     cols = bands * own
 
-    def copy(j):
+    def copy(j, l):
         part = pl.ds(j * STRIP, STRIP)
         return pltpu.make_async_copy(
-            tiles_hbm.at[:, :, part, :], tiles.at[:, :, part, :], sems.at[j]
+            tiles_hbm.at[l, :, part, :], tiles.at[l, :, part, :], sems.at[j, l]
         )
 
     for j in range(cells // STRIP):
-        copy(j).start()
+        for l in range(layers):
+            copy(j, l).start()
     order = pltpu.make_async_copy(order_hbm, order_ref, order_sem)
     order.start()
     if paired:
@@ -222,10 +223,10 @@
         strips = cells // STRIP
         for j in range(strips):
             part = slice(j * STRIP, (j + 1) * STRIP)
-            if first:
-                copy(j).wait()
             predicted = None
             for l in range(layers):
+                if first:
+                    copy(j, l).wait()
                 for k in range(span):
                     if first:
                         block = tiles[l, k, part, :].T
@@ -365,7 +366,7 @@
             pltpu.VMEM(near_tiles.shape, bf16),
             pltpu.SMEM((span,), jnp.int32),
             pltpu.SemaphoreType.DMA,
-            pltpu.SemaphoreType.DMA((cells // STRIP,)),
+            pltpu.SemaphoreType.DMA((cells // STRIP, layers)),
         ],
         compiler_params=pltpu.CompilerParams(vmem_limit_bytes=limit),
         name="steps",

time: 65.9 us -> 65.4 us (level)
  no operation moved by 1% of the time
where the time goes in v5:
time: 65.4 us; the launch traced here: 64.9 us
  Pallas kernels  30 us (46%)
  blocking collectives  15.4 us (24%)
  waiting for transfers between devices  7.76 us (12%)
  starting transfers between devices  7.43 us (11%)
  local copies, waits for them, and re-layouts  3.7 us (6%)
  between operations  0.68 us (1%)
    pallas_call x1, Pallas kernels, on_device(): pl.pallas_call(functools.partial(steps_kernel, bands=bands, own=own, rank...  26.6 us
    all_to_all x1, blocking collectives, on_device(): lax.all_to_all(result.reshape(bands, held, width), 'row', 0, 0, tiled=True)  15.4 us
    all_to_all x1, waiting for transfers between devices, on_device(): lax.all_to_all(packed.reshape(bands, held, width), 'row', 0, 0, tiled=True)  7.76 us
    all_to_all x1, starting transfers between devices, on_device(): lax.all_to_all(packed.reshape(bands, held, width), 'row', 0, 0, tiled=True)  7.43 us
    unnamed x6, local copies, waits for them, and re-layouts  2.63 us
    pallas_call x1, Pallas kernels, on_device(): pl.pallas_call(functools.partial(pack_kernel, own=own), out_shape=jax.Sha...  1.81 us
  transfers between devices with their start and end apart: 1, of which 1 were waited for; matrix products, arithmetic and copies ran while one was open for 2% of the time, Pallas kernels for 1%

profile of v5, /device:TPU:0, one launch (start us, length us, event | category | flops | bytes accessed | tf_op | source)
XLA Modules:
  0.0 64.9 jit_solution(7430999501928171610)
XLA Ops:
  0.6 1.8 %pack.1 = bf16[128,1536]{1,0:T(8,128)(2,1)} custom-call(bf16[2,64,1024]{2,1,0:T(8,128)(2,1)} %model_hbm.1, bf16[64,1024]{1,0:T(8,128)(2,1)} %data_hbm.1), custom_call_target="tpu_custom_call" | custom-call | tf_op jit(solution)/shard_map/pack/pallas_call | solution.py:303
  2.4 7.4 %all-to-all-start = ((bf16[16,8,1536]{2,1,0:T(8,128)(2,1)}), bf16[16,8,1536]{2,1,0:T(8,128)(2,1)S(1)}, u32[]{:S(2)}, u32[]{:S(2)}) async-start(bf16[16,8,1536]{2,1,0:T(8,128)(2,1)} %bitcast), calls=%async_computation | async-start | bytes 786432 | tf_op jit(solution)/shard_map/all_to_all | solution.py:323
  9.9 1.1 %copy.9 = f32[2,16,16,16]{3,2,1,0:T(8,128)S(1)} copy(f32[2,16,16,16]{2,3,1,0:T(8,128)} %bitcast.12) | data formatting | bytes 65536 | tf_op jit(solution)/shard_map/transpose | solution.py:345
  11.0 0.0 copy-start
  11.0 0.9 %copy-done = f32[2,16,16,16]{3,2,1,0:T(8,128)S(1)} copy-done((f32[2,16,16,16]{3,2,1,0:T(8,128)S(1)}, f32[2,16,16,16]{3,2,1,0:T(8,128)}, u32[]{:S(2)}) %copy-start) | copy-done | bytes 32792
  11.9 0.0 copy-start.1
  11.9 0.8 %copy-done.1 = bf16[2,1024,16]{1,2,0:T(8,128)(2,1)S(1)} copy-done((bf16[2,1024,16]{1,2,0:T(8,128)(2,1)S(1)}, bf16[2,1024,16]{1,2,0:T(8,128)(2,1)}, u32[]{:S(2)}) %copy-start.1) | copy-done | bytes 65560
  12.8 0.0 copy-start.2
  12.8 0.8 %copy-done.2 = bf16[2,1024,16]{1,2,0:T(8,128)(2,1)S(1)} copy-done((bf16[2,1024,16]{1,2,0:T(8,128)(2,1)S(1)}, bf16[2,1024,16]{1,2,0:T(8,128)(2,1)}, u32[]{:S(2)}) %copy-start.2) | copy-done | bytes 65560
  13.6 0.7 %tables.1 = (bf16[2,1024,128]{2,1,0:T(8,128)(2,1)S(1)}, bf16[2,1024,128]{2,1,0:T(8,128)(2,1)S(1)}, f32[2,256,128]{2,1,0:T(8,128)S(1)}, f32[2,256,128]{2,1,0:T(8,...) custom-call(bf16[2,16,1024]{2,1,0:T(8,128)(2,1)S(1)} %bitcast.15, ...), custom_call_target="tpu_custom_call" | custom-call | tf_op jit(solution)/shard_map/tables/pallas_call | solution.py:328
  14.3 7.8 %all-to-all-done = bf16[16,8,1536]{2,1,0:T(8,128)(2,1)S(1)} async-done(((bf16[16,8,1536]{2,1,0:T(8,128)(2,1)}), bf16[16,8,1536]{2,1,0:T(8,128)(2,1)S(1)}, u32[]{:S(2)}, u32[]{:S(2)}) %all-to-all-start) | async-done | bytes 393248 | tf_op jit(solution)/shard_map/all_to_all | solution.py:323
  22.0 26.6 %steps.1 = bf16[128,1536]{1,0:T(8,128)(2,1)S(1)} custom-call(s32[5]{0:T(128)} %order_hbm.1, bf16[128,1536]{1,0:T(8,128)(2,1)S(1)} %bitcast.10, bf16[2,5,1024,1024]{3,2,1,0:T(8,128)(2,1)} %tiles_hbm.1, bf16[2,1024,128]{2,1,0:T(8,128)(2,1)S(1)} %get-tuple-element.8.source_wide, bf16[2,1024,128]{2,1,0:T(8,128)(2,1)S(1)} %get-tuple-element.9.receiver_wide, ...), custom_call_target="tpu_custom_call" | custom-call | tf_op jit(solution)/shard_map/steps/pallas_call | solution.py:350
  48.6 15.4 %all_to_all.10 = bf16[16,8,1536]{2,1,0:T(8,128)(2,1)S(1)} all-to-all(bf16[16,8,1536]{2,1,0:T(8,128)(2,1)S(1)} %bitcast.11), channel_id=1, replica_groups=mesh['group'=2,'row'=16] {'row'}, dimensions={0} | all-to-all | bytes 786432 | tf_op jit(solution)/shard_map/all_to_all | solution.py:381
  64.0 0.9 %unpack.1 = (f32[2,64,1024]{2,1,0:T(8,128)}, f32[64,1024]{1,0:T(8,128)}) custom-call(bf16[128,1536]{1,0:T(8,128)(2,1)S(1)} %bitcast.9), custom_call_target="tpu_custom_call" | custom-call | tf_op jit(solution)/shard_map/unpack/pallas_call | solution.py:383
Async XLA Ops:
  2.4 19.6 %all-to-all-start = ((bf16[16,8,1536]{2,1,0:T(8,128)(2,1)}), bf16[16,8,1536]{2,1,0:T(8,128)(2,1)S(1)}, u32[]{:S(2)}, u32[]{:S(2)}) async-start(bf16[16,8,1536]{2,1,0:T(8,128)(2,1)} %bitcast), calls=%async_computation | async-start | bytes 786432 | tf_op jit(solution)/shard_map/all_to_all | solution.py:323
  11.0 1.0 %copy-start = (f32[2,16,16,16]{3,2,1,0:T(8,128)S(1)}, f32[2,16,16,16]{3,2,1,0:T(8,128)}, u32[]{:S(2)}) copy-start(f32[2,16,16,16]{3,2,1,0:T(8,128)} %param.11) | copy-start | bytes 98308
  11.9 0.8 %copy-start.1 = (bf16[2,1024,16]{1,2,0:T(8,128)(2,1)S(1)}, bf16[2,1024,16]{1,2,0:T(8,128)(2,1)}, u32[]{:S(2)}) copy-start(bf16[2,1024,16]{1,2,0:T(8,128)(2,1)} %param.10) | copy-start | bytes 196612
  12.8 0.8 %copy-start.2 = (bf16[2,1024,16]{1,2,0:T(8,128)(2,1)S(1)}, bf16[2,1024,16]{1,2,0:T(8,128)(2,1)}, u32[]{:S(2)}) copy-start(bf16[2,1024,16]{1,2,0:T(8,128)(2,1)} %param.9) | copy-start | bytes 196612
